TPU v7x, 128 devices: a whole 4x4x4 slice. The times are simulated.
128 devices in a mesh: slab: 64 (over z, y, x), col: 2 (over core).
Axes of the slice: x: 4, y: 4, z: 4, core: 2. Of those that a mesh axis runs over, the one named last changes fastest.
Arguments:
- coupling: float32 [64, 512, 512], P('slab', None, 'col'), as said below
- tile_pattern: int32 [64, 4, 4], P('slab', None, 'col'), may hold values from 0 to 1, as said below
- orbital_mass: float32 [64, 512], P('slab', 'col'), may hold values from 0.0001 to 0.05
- sources: float32 [64, 512, 256], P('slab', None, 'col'), may hold values from -0.3 to 0.3
Outputs:
- solution: float32 [64, 512, 256], P('slab', None, 'col')
Inputs may be any that keep to these rules, and one draw needn't show every extreme that they name: Each coupling block is symmetric and positive semidefinite. `tile_pattern`: in each slab every tile belongs to one group, and two tiles are linked exactly when they share a group, so each pattern is symmetric with ones on its diagonal.
All inputs are finite; a program needn't handle non-finite values.
Results may differ from a plain program's by a relative error of at most 0.0003.
Values sent between devices are 32-bit elements; how exact they have to be, the bound alone decides.
A program may use at most 128 MiB of HBM per device.

v0:
```python
import jax
import jax.numpy as jnp
from jax import lax
from jax.sharding import PartitionSpec as P

LEVELS = 6


leaf_limit = 128


def from_behind(shard, axis, by):
    size = lax.axis_size(axis)
    pairs = [(i, i + by) for i in range(size) if 0 <= i + by < size]
    return lax.ppermute(shard, axis, pairs)


def factor_inverse(matrix):
    width = matrix.shape[-1]
    if width <= leaf_limit:
        factor = jnp.linalg.cholesky(matrix)
        unit = jnp.eye(width, dtype=matrix.dtype)
        return lax.linalg.triangular_solve(factor, unit, left_side=True, lower=True)
    half_w = width // 2
    top_left = matrix[:half_w, :half_w]
    bottom_left = matrix[half_w:, :half_w]
    bottom_right = matrix[half_w:, half_w:]
    first_inv = factor_inverse(top_left)
    lower_part = jnp.dot(
        bottom_left,
        first_inv.T,
        precision=lax.Precision.HIGHEST,
        preferred_element_type=jnp.float32,
    )
    schur_part = bottom_right - jnp.dot(
        lower_part,
        lower_part.T,
        precision=lax.Precision.HIGHEST,
        preferred_element_type=jnp.float32,
    )
    second_inv = factor_inverse(schur_part)
    cross = -jnp.dot(
        second_inv,
        jnp.dot(
            lower_part,
            first_inv,
            precision=lax.Precision.HIGHEST,
            preferred_element_type=jnp.float32,
        ),
        precision=lax.Precision.HIGHEST,
        preferred_element_type=jnp.float32,
    )
    upper_row = jnp.concatenate(
        [first_inv, jnp.zeros((half_w, width - half_w), jnp.float32)], axis=1
    )
    lower_row = jnp.concatenate([cross, second_inv], axis=1)
    return jnp.concatenate([upper_row, lower_row], axis=0)


def solve_spd(matrix, rhs):
    inverse = factor_inverse(matrix)
    inner = jnp.dot(
        inverse, rhs, precision=lax.Precision.HIGHEST, preferred_element_type=jnp.float32
    )
    return jnp.dot(
        inverse.T, inner, precision=lax.Precision.HIGHEST, preferred_element_type=jnp.float32
    )


def on_device(coupling, tile_pattern, orbital_mass, sources):
    width = coupling.shape[1]
    half = coupling.shape[2]
    tiles_row = tile_pattern.shape[1]
    tiles_col = tile_pattern.shape[2]
    tile_width = width // tiles_row
    column = lax.axis_index("col")
    slab_index = lax.axis_index("slab")
    slab_count = lax.axis_size("slab")
    tile_mask = jnp.broadcast_to(
        tile_pattern[0][:, None, :, None].astype(jnp.float32),
        (tiles_row, tile_width, tiles_col, tile_width),
    ).reshape(width, half)
    row_ids = lax.broadcasted_iota(jnp.int32, (width, half), 0)
    col_ids = lax.broadcasted_iota(jnp.int32, (width, half), 1) + column * half
    unit_panel = (row_ids == col_ids).astype(jnp.float32)
    bond_panel = unit_panel + tile_mask * coupling[0]
    prior_panel = from_behind(bond_panel, "slab", 1)
    keep_upper = (slab_index < slab_count - 1).astype(jnp.float32)
    lower_panel = -prior_panel
    upper_panel = -bond_panel * keep_upper
    diag_panel = bond_panel + prior_panel + unit_panel * orbital_mass[0][None, :]
    source_panel = sources[0]
    for level_num in range(LEVELS):
        stride = 2**level_num
        full_diag, full_lower, full_upper = (
            lax.all_gather(diag_panel, "col", axis=1, tiled=True),
            lax.all_gather(lower_panel, "col", axis=1, tiled=True),
            lax.all_gather(upper_panel, "col", axis=1, tiled=True),
        )
        solved = solve_spd(
            full_diag, jnp.concatenate([upper_panel, lower_panel, source_panel], axis=1)
        )
        from_below = from_behind(solved, "slab", stride)
        from_above = from_behind(solved, "slab", -stride)
        below_prod = jnp.dot(
            full_lower,
            from_below,
            precision=lax.Precision.HIGHEST,
            preferred_element_type=jnp.float32,
        )
        above_prod = jnp.dot(
            full_upper,
            from_above,
            precision=lax.Precision.HIGHEST,
            preferred_element_type=jnp.float32,
        )
        diag_panel = diag_panel - below_prod[:, :half] - above_prod[:, half : 2 * half]
        lower_panel = -below_prod[:, half : 2 * half]
        upper_panel = -above_prod[:, :half]
        source_panel = source_panel - below_prod[:, 2 * half :] - above_prod[:, 2 * half :]
    final_diag = lax.all_gather(diag_panel, "col", axis=1, tiled=True)
    solution = solve_spd(final_diag, source_panel)
    return solution[None]


def solution(mesh):
    placed = (
        P("slab", None, "col"),
        P("slab", None, "col"),
        P("slab", "col"),
        P("slab", None, "col"),
    )
    return jax.shard_map(
        on_device, mesh=mesh, in_specs=placed, out_specs=P("slab", None, "col"), check_vma=False
    )
```

profile of v0, /device:TPU:31, one launch (start us, length us, event | category | flops | bytes accessed | tf_op | source)
XLA Modules:
  0.0 1240.8 jit_solution(6250302416313624978)
XLA Ops:
  11.9 11.6 collective-permute-done
  25.4 14.5 %all-gather.22.cloned.1.call-done = f32[512,512]{0,1:T(8,128)} async-done(((f32[512,256]{0,1:T(8,128)}), f32[512,512]{0,1:T(8,128)}) %all-gather.22.cloned.1.call-update) | async-done | bytes 1048592 | tf_op jit(solution)/shard_map/all_gather | solution.py:96
  41.9 11.7 cholesky.434
  67.6 11.7 cholesky.445
  80.7 10.0 custom-call.33
  92.9 11.7 cholesky.456
  117.0 23.4 %cholesky.467 = f32[128,128]{1,0:T(8,128)S(1)} custom-call(f32[128,128]{1,0:T(8,128)S(1)} %fusion.254), custom_call_target="Cholesky" | custom-call | tf_op jit(solution)/shard_map/jit(cholesky)/cholesky | solution.py:21
  164.5 27.0 %collective-permute-done.1 = f32[512,640]{1,0:T(8,128)S(1)} collective-permute-done((f32[512,640]{1,0:T(8,128)}, f32[512,640]{1,0:T(8,128)S(1)}, u32[]{:S(2)}, u32[]{:S(2)}) %collective-permute-start.1) | collective-permute-done | bytes 1310752 | tf_op jit(solution)/shard_map/ppermute | solution.py:15
  209.3 12.4 %all-gather.28.cloned.1.call-done = f32[512,512]{0,1:T(8,128)} async-done(((f32[512,256]{0,1:T(8,128)}), f32[512,512]{0,1:T(8,128)}) %all-gather.28.cloned.1.call-update) | async-done | bytes 1048592 | tf_op jit(solution)/shard_map/all_gather | solution.py:96
  223.6 11.7 cholesky.478
  249.4 11.7 cholesky.489
  274.6 11.7 cholesky.500
  298.7 12.1 cholesky.511
  336.4 26.9 %collective-permute-done.3 = f32[512,640]{1,0:T(8,128)S(1)} collective-permute-done((f32[512,640]{1,0:T(8,128)}, f32[512,640]{1,0:T(8,128)S(1)}, u32[]{:S(2)}, u32[]{:S(2)}) %collective-permute-start.3) | collective-permute-done | bytes 1310752 | tf_op jit(solution)/shard_map/ppermute | solution.py:15
  369.1 23.3 %collective-permute-done.4 = f32[512,640]{1,0:T(8,128)} collective-permute-done((f32[512,640]{1,0:T(8,128)}, f32[512,640]{1,0:T(8,128)}, u32[]{:S(2)}, u32[]{:S(2)}) %collective-permute-start.4) | collective-permute-done | bytes 1310752 | tf_op jit(solution)/shard_map/ppermute | solution.py:15
  403.0 12.8 %all-gather.34.cloned.1.call-done = f32[512,512]{0,1:T(8,128)} async-done(((f32[512,256]{0,1:T(8,128)}), f32[512,512]{0,1:T(8,128)}) %all-gather.34.cloned.1.call-update) | async-done | bytes 1048592 | tf_op jit(solution)/shard_map/all_gather | solution.py:96
  417.7 11.7 cholesky.522
  443.3 11.7 cholesky.533
  456.3 10.2 custom-call.41
  468.7 11.7 cholesky.544
  492.7 11.9 cholesky.555
  528.7 27.0 %collective-permute-done.5 = f32[512,640]{1,0:T(8,128)S(1)} collective-permute-done((f32[512,640]{1,0:T(8,128)}, f32[512,640]{1,0:T(8,128)S(1)}, u32[]{:S(2)}, u32[]{:S(2)}) %collective-permute-start.5) | collective-permute-done | bytes 1310752 | tf_op jit(solution)/shard_map/ppermute | solution.py:15
  572.7 12.3 all-gather.40.cloned.1.call-done
  586.9 11.7 cholesky.566
  612.6 11.7 cholesky.577
  637.9 11.7 cholesky.588
  662.0 12.1 cholesky.599
  699.8 26.8 %collective-permute-done.7 = f32[512,640]{1,0:T(8,128)S(1)} collective-permute-done((f32[512,640]{1,0:T(8,128)}, f32[512,640]{1,0:T(8,128)S(1)}, u32[]{:S(2)}, u32[]{:S(2)}) %collective-permute-start.7) | collective-permute-done | bytes 1310752 | tf_op jit(solution)/shard_map/ppermute | solution.py:15
  732.4 23.3 %collective-permute-done.8 = f32[512,640]{1,0:T(8,128)} collective-permute-done((f32[512,640]{1,0:T(8,128)}, f32[512,640]{1,0:T(8,128)}, u32[]{:S(2)}, u32[]{:S(2)}) %collective-permute-start.8) | collective-permute-done | bytes 1310752 | tf_op jit(solution)/shard_map/ppermute | solution.py:15
  766.2 12.9 %all-gather.46.cloned.1.call-done = f32[512,512]{0,1:T(8,128)} async-done(((f32[512,256]{0,1:T(8,128)}), f32[512,512]{0,1:T(8,128)}) %all-gather.46.cloned.1.call-update) | async-done | bytes 1048592 | tf_op jit(solution)/shard_map/all_gather | solution.py:96
  781.0 11.7 cholesky.610
  806.7 11.7 cholesky.621
  819.7 10.2 custom-call.49
  832.1 11.7 cholesky.632
  856.1 11.9 cholesky.643
  891.3 26.8 %collective-permute-done.9 = f32[512,640]{1,0:T(8,128)S(1)} collective-permute-done((f32[512,640]{1,0:T(8,128)}, f32[512,640]{1,0:T(8,128)S(1)}, u32[]{:S(2)}, u32[]{:S(2)}) %collective-permute-start.9) | collective-permute-done | bytes 1310752 | tf_op jit(solution)/shard_map/ppermute | solution.py:15
  935.8 12.6 %all-gather.52.cloned.1.call-done = f32[512,512]{0,1:T(8,128)} async-done(((f32[512,256]{0,1:T(8,128)}), f32[512,512]{0,1:T(8,128)}) %all-gather.52.cloned.1.call-update) | async-done | bytes 1048592 | tf_op jit(solution)/shard_map/all_gather | solution.py:96
  950.3 11.7 cholesky.654
  976.1 11.7 cholesky.665
  1001.5 11.7 cholesky.676
  1025.7 11.9 cholesky.687
  1063.2 26.4 %collective-permute-done.11 = f32[512,640]{1,0:T(8,128)S(1)} collective-permute-done((f32[512,640]{1,0:T(8,128)}, f32[512,640]{1,0:T(8,128)S(1)}, u32[]{:S(2)}, u32[]{:S(2)}) %collective-permute-start.11) | collective-permute-done | bytes 1310752 | tf_op jit(solution)/shard_map/ppermute | solution.py:15
  1099.8 13.0 %all-gather.56.cloned.1.call-done = f32[512,512]{0,1:T(8,128)} async-done(((f32[512,256]{0,1:T(8,128)}), f32[512,512]{0,1:T(8,128)}) %all-gather.56.cloned.1.call-update) | async-done | bytes 1048592 | tf_op jit(solution)/shard_map/all_gather | solution.py:121
  1114.6 11.7 cholesky.698
  1140.3 11.9 cholesky.709
  1171.0 13.2 %cholesky.720 = f32[128,128]{1,0:T(8,128)} custom-call(f32[128,128]{1,0:T(8,128)} %fusion.208), custom_call_target="Cholesky" | custom-call | tf_op jit(solution)/shard_map/jit(cholesky)/cholesky | solution.py:21
  1187.8 11.5 custom-call.58
  1205.8 11.7 cholesky.731
  (542 shorter events, 530.3 us)
Async XLA Ops:
  6.5 33.4 %all-gather.22.cloned.1.call-start = ((), (), s32[]{:S(2)}) async-start(), calls=%async_computation.1 | async-start | bytes 1572864 | tf_op jit(solution)/shard_map/all_gather | solution.py:96
  8.8 143.8 %copy-start.20 = (f32[512,256]{0,1:T(8,128)}, f32[512,256]{0,1:T(8,128)S(1)}, u32[]{:S(2)}) copy-start(f32[512,256]{0,1:T(8,128)S(1)} %get-tuple-element.6) | copy-start | bytes 1572868
  8.8 14.7 %collective-permute-start = (f32[512,256]{0,1:T(8,128)S(1)}, f32[512,256]{0,1:T(8,128)S(1)}, u32[]{:S(2)}, u32[]{:S(2)}) collective-permute-start(f32[512,256]{0,1:T(8,128)S(1)} %get-tuple-element.8), channel_id=1, source_target_pairs={{0,2},{2,4},{4,6},{6,8},{8,10},{10,12},{12,14},{14,16},{16,18},{18... | collective-permute-start | bytes 1572872 | tf_op jit(solution)/shard_map/ppermute | solution.py:15
  24.6 139.9 %all-gather.20.cloned.1.call-start = ((), (), s32[]{:S(2)}) async-start(), calls=%async_computation | async-start | bytes 1572864 | tf_op jit(solution)/shard_map/all_gather | solution.py:97
  25.4 172.0 %all-gather.24.cloned.1.call-start = ((), (), s32[]{:S(2)}) async-start(), calls=%async_computation.2 | async-start | bytes 1572864 | tf_op jit(solution)/shard_map/all_gather | solution.py:98
  40.0 51.4 %copy-start.28 = (f32[512,512]{0,1:T(8,128)S(1)}, f32[512,512]{0,1:T(8,128)}, u32[]{:S(2)}) copy-start(f32[512,512]{0,1:T(8,128)} %all-gather.22.cloned.1.call-done) | copy-start | bytes 3145732
  116.6 36.1 %copy-start.10 = (f32[512,256]{0,1:T(8,128)S(1)}, f32[512,256]{0,1:T(8,128)}, u32[]{:S(2)}) copy-start(f32[512,256]{0,1:T(8,128)} %get-tuple-element.30) | copy-start | bytes 1572868
  159.1 32.4 %collective-permute-start.1 = (f32[512,640]{1,0:T(8,128)}, f32[512,640]{1,0:T(8,128)S(1)}, u32[]{:S(2)}, u32[]{:S(2)}) collective-permute-start(f32[512,640]{1,0:T(8,128)} %fusion.93), channel_id=1, source_target_pairs={{0,2},{2,4},{4,6},{6,8},{8,10},{10,12},{12,14},{14,16},{16,18},{18... | collective-permute-start | bytes 3932168 | tf_op jit(solution)/shard_map/ppermute | solution.py:15
  162.2 36.3 %collective-permute-start.2 = (f32[512,640]{1,0:T(8,128)}, f32[512,640]{1,0:T(8,128)}, u32[]{:S(2)}, u32[]{:S(2)}) collective-permute-start(f32[512,640]{1,0:T(8,128)} %fusion.93), channel_id=1, source_target_pairs={{2,0},{4,2},{6,4},{8,6},{10,8},{12,10},{14,12},{16,14},{18,16},{20... | collective-permute-start | bytes 3932168 | tf_op jit(solution)/shard_map/ppermute | solution.py:15
  164.5 57.3 %all-gather.28.cloned.1.call-start = ((), (), s32[]{:S(2)}) async-start(), calls=%async_computation.4 | async-start | bytes 1572864 | tf_op jit(solution)/shard_map/all_gather | solution.py:96
  208.3 128.2 %all-gather.26.cloned.1.call-start = ((), (), s32[]{:S(2)}) async-start(), calls=%async_computation.3 | async-start | bytes 1572864 | tf_op jit(solution)/shard_map/all_gather | solution.py:97
  208.9 160.3 %all-gather.30.cloned.1.call-start = ((), (), s32[]{:S(2)}) async-start(), calls=%async_computation.5 | async-start | bytes 1572864 | tf_op jit(solution)/shard_map/all_gather | solution.py:98
  221.7 51.3 %copy-start.23 = (f32[512,512]{0,1:T(8,128)S(1)}, f32[512,512]{0,1:T(8,128)}, u32[]{:S(2)}) copy-start(f32[512,512]{0,1:T(8,128)} %all-gather.28.cloned.1.call-done) | copy-start | bytes 3145732
  298.3 24.8 %copy-start.11 = (f32[512,256]{1,0:T(8,128)S(1)}, f32[512,256]{1,0:T(8,128)}, u32[]{:S(2)}) copy-start(f32[512,256]{1,0:T(8,128)} %get-tuple-element.26) | copy-start | bytes 1572868
  298.3 24.8 %copy-start.16 = (f32[512,256]{1,0:T(8,128)S(1)}, f32[512,256]{1,0:T(8,128)}, u32[]{:S(2)}) copy-start(f32[512,256]{1,0:T(8,128)} %get-tuple-element.28) | copy-start | bytes 1572868
  329.6 33.8 %collective-permute-start.3 = (f32[512,640]{1,0:T(8,128)}, f32[512,640]{1,0:T(8,128)S(1)}, u32[]{:S(2)}, u32[]{:S(2)}) collective-permute-start(f32[512,640]{1,0:T(8,128)} %fusion.94), channel_id=1, source_target_pairs={{0,4},{2,6},{4,8},{6,10},{8,12},{10,14},{12,16},{14,18},{16,20},{1... | collective-permute-start | bytes 3932168 | tf_op jit(solution)/shard_map/ppermute | solution.py:15
  333.6 58.9 %collective-permute-start.4 = (f32[512,640]{1,0:T(8,128)}, f32[512,640]{1,0:T(8,128)}, u32[]{:S(2)}, u32[]{:S(2)}) collective-permute-start(f32[512,640]{1,0:T(8,128)} %fusion.94), channel_id=1, source_target_pairs={{4,0},{6,2},{8,4},{10,6},{12,8},{14,10},{16,12},{18,14},{20,16},{2... | collective-permute-start | bytes 3932168 | tf_op jit(solution)/shard_map/ppermute | solution.py:15
  336.4 79.4 %all-gather.34.cloned.1.call-start = ((), (), s32[]{:S(2)}) async-start(), calls=%async_computation.7 | async-start | bytes 1572864 | tf_op jit(solution)/shard_map/all_gather | solution.py:96
  402.1 126.6 %all-gather.32.cloned.1.call-start = ((), (), s32[]{:S(2)}) async-start(), calls=%async_computation.6 | async-start | bytes 1572864 | tf_op jit(solution)/shard_map/all_gather | solution.py:97
  402.5 28.2 %copy-start.6 = (f32[512,128]{0,1:T(8,128)}, f32[512,128]{0,1:T(8,128)S(1)}, u32[]{:S(2)}) copy-start(f32[512,128]{0,1:T(8,128)S(1)} %subtract_subtract_fusion.8) | copy-start | bytes 786436
  402.8 158.7 %all-gather.36.cloned.1.call-start = ((), (), s32[]{:S(2)}) async-start(), calls=%async_computation.8 | async-start | bytes 1572864 | tf_op jit(solution)/shard_map/all_gather | solution.py:98
  415.8 51.4 %copy-start.24 = (f32[512,512]{0,1:T(8,128)S(1)}, f32[512,512]{0,1:T(8,128)}, u32[]{:S(2)}) copy-start(f32[512,512]{0,1:T(8,128)} %all-gather.34.cloned.1.call-done) | copy-start | bytes 3145732
  523.3 32.4 %collective-permute-start.5 = (f32[512,640]{1,0:T(8,128)}, f32[512,640]{1,0:T(8,128)S(1)}, u32[]{:S(2)}, u32[]{:S(2)}) collective-permute-start(f32[512,640]{1,0:T(8,128)} %fusion.95), channel_id=1, source_target_pairs={{0,8},{2,10},{4,12},{6,14},{8,16},{10,18},{12,20},{14,22},{16,24},... | collective-permute-start | bytes 3932168 | tf_op jit(solution)/shard_map/ppermute | solution.py:15
  526.4 35.1 %collective-permute-start.6 = (f32[512,640]{1,0:T(8,128)}, f32[512,640]{1,0:T(8,128)}, u32[]{:S(2)}, u32[]{:S(2)}) collective-permute-start(f32[512,640]{1,0:T(8,128)} %fusion.95), channel_id=1, source_target_pairs={{8,0},{10,2},{12,4},{14,6},{16,8},{18,10},{20,12},{22,14},{24,16},... | collective-permute-start | bytes 3932168 | tf_op jit(solution)/shard_map/ppermute | solution.py:15
  528.6 56.4 %all-gather.40.cloned.1.call-start = ((), (), s32[]{:S(2)}) async-start(), calls=%async_computation.10 | async-start | bytes 1572864 | tf_op jit(solution)/shard_map/all_gather | solution.py:96
  571.1 128.7 %all-gather.38.cloned.1.call-start = ((), (), s32[]{:S(2)}) async-start(), calls=%async_computation.9 | async-start | bytes 1572864 | tf_op jit(solution)/shard_map/all_gather | solution.py:97
  572.3 160.2 %all-gather.42.cloned.1.call-start = ((), (), s32[]{:S(2)}) async-start(), calls=%async_computation.11 | async-start | bytes 1572864 | tf_op jit(solution)/shard_map/all_gather | solution.py:98
  585.0 51.3 %copy-start.25 = (f32[512,512]{0,1:T(8,128)S(1)}, f32[512,512]{0,1:T(8,128)}, u32[]{:S(2)}) copy-start(f32[512,512]{0,1:T(8,128)} %all-gather.40.cloned.1.call-done) | copy-start | bytes 3145732
  661.5 24.8 %copy-start.13 = (f32[512,256]{1,0:T(8,128)S(1)}, f32[512,256]{1,0:T(8,128)}, u32[]{:S(2)}) copy-start(f32[512,256]{1,0:T(8,128)} %get-tuple-element.18) | copy-start | bytes 1572868
  661.6 24.8 %copy-start.18 = (f32[512,256]{1,0:T(8,128)S(1)}, f32[512,256]{1,0:T(8,128)}, u32[]{:S(2)}) copy-start(f32[512,256]{1,0:T(8,128)} %get-tuple-element.20) | copy-start | bytes 1572868
  692.8 33.8 %collective-permute-start.7 = (f32[512,640]{1,0:T(8,128)}, f32[512,640]{1,0:T(8,128)S(1)}, u32[]{:S(2)}, u32[]{:S(2)}) collective-permute-start(f32[512,640]{1,0:T(8,128)} %fusion.96), channel_id=1, source_target_pairs={{0,16},{2,18},{4,20},{6,22},{8,24},{10,26},{12,28},{14,30},{16,32}... | collective-permute-start | bytes 3932168 | tf_op jit(solution)/shard_map/ppermute | solution.py:15
  696.9 58.9 %collective-permute-start.8 = (f32[512,640]{1,0:T(8,128)}, f32[512,640]{1,0:T(8,128)}, u32[]{:S(2)}, u32[]{:S(2)}) collective-permute-start(f32[512,640]{1,0:T(8,128)} %fusion.96), channel_id=1, source_target_pairs={{16,0},{18,2},{20,4},{22,6},{24,8},{26,10},{28,12},{30,14},{32,16}... | collective-permute-start | bytes 3932168 | tf_op jit(solution)/shard_map/ppermute | solution.py:15
  699.7 79.4 %all-gather.46.cloned.1.call-start = ((), (), s32[]{:S(2)}) async-start(), calls=%async_computation.13 | async-start | bytes 1572864 | tf_op jit(solution)/shard_map/all_gather | solution.py:96
  765.4 125.9 %all-gather.44.cloned.1.call-start = ((), (), s32[]{:S(2)}) async-start(), calls=%async_computation.12 | async-start | bytes 1572864 | tf_op jit(solution)/shard_map/all_gather | solution.py:97
  765.8 28.2 %copy-start.8 = (f32[512,128]{0,1:T(8,128)}, f32[512,128]{0,1:T(8,128)S(1)}, u32[]{:S(2)}) copy-start(f32[512,128]{0,1:T(8,128)S(1)} %subtract_subtract_fusion.6) | copy-start | bytes 786436
  766.0 157.9 %all-gather.48.cloned.1.call-start = ((), (), s32[]{:S(2)}) async-start(), calls=%async_computation.14 | async-start | bytes 1572864 | tf_op jit(solution)/shard_map/all_gather | solution.py:98
  779.2 51.4 %copy-start.26 = (f32[512,512]{0,1:T(8,128)S(1)}, f32[512,512]{0,1:T(8,128)}, u32[]{:S(2)}) copy-start(f32[512,512]{0,1:T(8,128)} %all-gather.46.cloned.1.call-done) | copy-start | bytes 3145732
  886.6 31.4 %collective-permute-start.9 = (f32[512,640]{1,0:T(8,128)}, f32[512,640]{1,0:T(8,128)S(1)}, u32[]{:S(2)}, u32[]{:S(2)}) collective-permute-start(f32[512,640]{1,0:T(8,128)} %fusion.97), channel_id=1, source_target_pairs={{0,32},{2,34},{4,36},{6,38},{8,40},{10,42},{12,44},{14,46},{16,48}... | collective-permute-start | bytes 3932168 | tf_op jit(solution)/shard_map/ppermute | solution.py:15
  889.9 34.0 %collective-permute-start.10 = (f32[512,640]{1,0:T(8,128)}, f32[512,640]{1,0:T(8,128)}, u32[]{:S(2)}, u32[]{:S(2)}) collective-permute-start(f32[512,640]{1,0:T(8,128)} %fusion.97), channel_id=1, source_target_pairs={{32,0},{34,2},{36,4},{38,6},{40,8},{42,10},{44,12},{46,14},{48,16}... | collective-permute-start | bytes 3932168 | tf_op jit(solution)/shard_map/ppermute | solution.py:15
  891.2 57.2 %all-gather.52.cloned.1.call-start = ((), (), s32[]{:S(2)}) async-start(), calls=%async_computation.16 | async-start | bytes 1572864 | tf_op jit(solution)/shard_map/all_gather | solution.py:96
  933.5 129.6 %all-gather.50.cloned.1.call-start = ((), (), s32[]{:S(2)}) async-start(), calls=%async_computation.15 | async-start | bytes 1572864 | tf_op jit(solution)/shard_map/all_gather | solution.py:97
  935.4 157.7 %all-gather.54.cloned.1.call-start = ((), (), s32[]{:S(2)}) async-start(), calls=%async_computation.17 | async-start | bytes 1572864 | tf_op jit(solution)/shard_map/all_gather | solution.py:98
  948.4 51.5 %copy-start.27 = (f32[512,512]{0,1:T(8,128)S(1)}, f32[512,512]{0,1:T(8,128)}, u32[]{:S(2)}) copy-start(f32[512,512]{0,1:T(8,128)} %all-gather.52.cloned.1.call-done) | copy-start | bytes 3145732
  1025.3 24.7 %copy-start.15 = (f32[512,256]{1,0:T(8,128)S(1)}, f32[512,256]{1,0:T(8,128)}, u32[]{:S(2)}) copy-start(f32[512,256]{1,0:T(8,128)} %get-tuple-element.10) | copy-start | bytes 1572868
  1056.5 33.0 %collective-permute-start.11 = (f32[512,640]{1,0:T(8,128)}, f32[512,640]{1,0:T(8,128)S(1)}, u32[]{:S(2)}, u32[]{:S(2)}) collective-permute-start(f32[512,640]{1,0:T(8,128)} %fusion.98), channel_id=1, source_target_pairs={{0,64},{2,66},{4,68},{6,70},{8,72},{10,74},{12,76},{14,78},{16,80}... | collective-permute-start | bytes 3932168 | tf_op jit(solution)/shard_map/ppermute | solution.py:15
  1061.4 33.6 %collective-permute-start.12 = (f32[512,640]{1,0:T(8,128)}, f32[512,640]{1,0:T(8,128)}, u32[]{:S(2)}, u32[]{:S(2)}) collective-permute-start(f32[512,640]{1,0:T(8,128)} %fusion.98), channel_id=1, source_target_pairs={{64,0},{66,2},{68,4},{70,6},{72,8},{74,10},{76,12},{78,14},{80,16}... | collective-permute-start | bytes 3932168 | tf_op jit(solution)/shard_map/ppermute | solution.py:15
  1062.7 50.1 %all-gather.56.cloned.1.call-start = ((), (), s32[]{:S(2)}) async-start(), calls=%async_computation.18 | async-start | bytes 1572864 | tf_op jit(solution)/shard_map/all_gather | solution.py:121
  1202.4 26.6 %copy-start.29 = (f32[128,128]{1,0:T(8,128)S(1)}, f32[128,128]{1,0:T(8,128)}, u32[]{:S(2)}) copy-start(f32[128,128]{1,0:T(8,128)} %fusion.401) | copy-start | bytes 196612
  (18 other events, 190.6 us)
Sparse Core Ops, SparseCore 0:
  24.8 15.1 all-gather.21
  41.6 13.2 all-gather.19
  164.6 13.9 all-gather.23
  208.4 13.3 all-gather.27
  223.2 13.1 all-gather.25
  336.5 14.2 all-gather.29
  402.2 13.5 all-gather.33
  417.5 13.2 all-gather.31
  528.7 14.2 all-gather.35
  571.2 13.7 all-gather.39
  586.7 13.2 all-gather.37
  699.9 14.4 all-gather.41
  765.5 13.5 all-gather.45
  780.7 13.1 all-gather.43
  891.3 15.2 all-gather.47
  933.6 14.6 all-gather.51
  949.9 13.1 all-gather.49
  1062.8 15.4 all-gather.53
  1100.0 12.8 all-gather.55
where the time goes:
time: 1250 us; the launch traced here: 1240 us
  other arithmetic  694 us (56%)
  waiting for transfers between devices  314 us (25%)
  matrix products  142 us (11%)
  starting transfers between devices  40.7 us (3%)
  local copies, waits for them, and re-layouts  34.1 us (3%)
  between operations  16.6 us (1%)
    another operation x84, other arithmetic, factor_inverse(): factor = jnp.linalg.cholesky(matrix)  363 us
    another operation x56, other arithmetic, factor_inverse(): return lax.linalg.triangular_solve(factor, unit, left_side=True, lower=True)  297 us
    ppermute x13, waiting for transfers between devices, from_behind(): return lax.ppermute(shard, axis, pairs)  222 us
    all_gather x6, waiting for transfers between devices, on_device(): lax.all_gather(diag_panel, 'col', axis=1, tiled=True)  77.5 us
    ppermute x13, starting transfers between devices, from_behind(): return lax.ppermute(shard, axis, pairs)  38 us
    dot_general x6, matrix products, on_device(): jnp.dot(full_upper, from_above, precision=lax.Precision.HIGHEST, preferre...  25.6 us
  transfers between devices with their start and end apart: 32, of which 18 were waited for; matrix products, arithmetic and copies ran while one was open for 56% of the time, Pallas kernels for 0%

commit v1 on v0

v1 whole, which is shorter than its diff:
```python
import functools

import jax
import jax.numpy as jnp
from jax import lax
from jax.experimental import pallas as pl
from jax.experimental.pallas import tpu as pltpu
from jax.sharding import PartitionSpec as P

F32 = jnp.float32
N = 512
H = 256
T = 128
M = 256
NT = (((1,), (1,)), ((), ()))
NN = (((1,), (0,)), ((), ()))
TILES = ((0, 0), (1, 0), (1, 1), (2, 0), (3, 0), (2, 1), (3, 1), (2, 2), (3, 2), (3, 3))
PIECES = ((0, 3), (3, 4), (7, 3))
MESH = pl.DeviceIdType.MESH


def dot(a, b, dims=NT):
    return lax.dot_general(
        a, b, dims, precision=lax.Precision.HIGHEST, preferred_element_type=F32
    )


def leaf(block, scr):
    rows = [block[8 * i : 8 * i + 8, :] for i in range(16)]
    lane = lax.broadcasted_iota(jnp.int32, (8, T), 1)
    sub = lax.broadcasted_iota(jnp.int32, (8, T), 0)
    out = []
    for J in range(16):
        b = (J % 2) * 9
        own = (lane >= 8 * J) & (lane < 8 * J + 8)
        for j in range(8):
            scr[b + j] = jnp.broadcast_to(rows[J][:, 8 * J + j : 8 * J + j + 1], (8, T))
        scr[b + 8] = jnp.where(own, jnp.where(lane == sub + 8 * J, 1.0, 0.0), rows[J])
        R = [jnp.broadcast_to(scr[b + 8, i : i + 1, :], (8, T)) for i in range(8)]
        E = [[None] * 8 for _ in range(8)]
        for i in range(8):
            for j in range(i + 1):
                E[i][j] = E[j][i] = jnp.broadcast_to(scr[b + j, i : i + 1, :], (8, T))
        V = [None] * 8
        for j in range(0, 8, 2):
            a, c, e = E[j][j], E[j][j + 1], E[j + 1][j + 1]
            q = 1.0 / (a * e - c * c)
            r = c * (1.0 / a)
            V[j] = R[j] * lax.rsqrt(a)
            V[j + 1] = (R[j + 1] - r * R[j]) * lax.rsqrt(e - c * r)
            ia, ic, ie = e * q, c * q, a * q
            R[j], R[j + 1] = ia * R[j] - ic * R[j + 1], ie * R[j + 1] - ic * R[j]
            for k in range(j + 2, 8):
                E[j][k], E[j + 1][k] = (
                    ia * E[j][k] - ic * E[j + 1][k],
                    ie * E[j + 1][k] - ic * E[j][k],
                )
            for i in range(8):
                if i in (j, j + 1):
                    continue
                m0, m1 = E[i][j], E[i][j + 1]
                R[i] = R[i] - (m0 * R[j] + m1 * R[j + 1])
                for k in range(j + 2, 8):
                    if i < j or k >= i:
                        E[i][k] = E[i][k] - (m0 * E[j][k] + m1 * E[j + 1][k])
            for i in range(j + 2, 8):
                for k in range(j + 2, i):
                    E[i][k] = E[k][i]
        for i in range(J + 1, 16):
            t = None
            for k in range(8):
                c = jnp.broadcast_to(rows[i][:, 8 * J + k : 8 * J + k + 1], (8, T)) * R[k]
                t = c if t is None else t + c
            rows[i] = jnp.where(own, 0.0, rows[i]) - t
        z = V[0]
        for r in range(1, 8):
            z = jnp.where(sub == r, V[r], z)
        out.append(jnp.where(lane <= sub + 8 * J, z, 0.0))
    return jnp.concatenate(out, 0)


def kernel(
    slabs,
    levels,
    brow,
    srct,
    mrow,
    out,
    recvP,
    recvQ,
    sibQ,
    recvR,
    sibR,
    VY,
    O,
    VX,
    VR,
    RT,
    D,
    DW,
    T2,
    G,
    W,
    scr,
    mb,
    sendQ,
    sendP,
    sendR,
    i_send,
    i_recv,
    n_send,
    n_recv,
    f_send,
    f_recv,
    v_send,
    v_recv,
    q_send,
    q_recv,
    qf_send,
    qf_recv,
    p_send,
    p_recv,
    r_send,
    r_recv,
    rf_send,
    rf_recv,
):
    s = lax.axis_index("slab")
    c = lax.axis_index("col")
    sgn = 2 * c - 1
    sib = 1 - c

    def inside(t):
        return (t >= 0) & (t < slabs)

    def remote(src, dst, ss, rs, slab, col):
        return pltpu.make_async_remote_copy(
            src_ref=src,
            dst_ref=dst,
            send_sem=ss,
            recv_sem=rs,
            device_id={"slab": slab, "col": col},
            device_id_type=MESH,
        )

    barrier = pltpu.get_barrier_semaphore()
    pl.semaphore_signal(barrier, inc=1, device_id={"slab": s, "col": sib}, device_id_type=MESH)
    count = 1
    for k in range(levels):
        peer = s + sgn * 2**k
        here = inside(peer)
        count = count + here.astype(jnp.int32)

        @pl.when(here)
        def _():
            pl.semaphore_signal(
                barrier, inc=1, device_id={"slab": peer, "col": sib}, device_id_type=MESH
            )

    pl.semaphore_wait(barrier, count)

    first = recvP.at[0]
    own_rt = pl.ds(pl.multiple_of(c * T, T), T)
    RT[own_rt, :] = srct[...]
    to_sib = functools.partial(remote, slab=s, col=sib)
    cp_m = to_sib(mrow, mb, i_send.at[0], i_recv.at[0])
    cp_r = to_sib(srct, RT.at[own_rt], i_send.at[1], i_recv.at[1])
    low, high = pl.ds(0, H), pl.ds(H, H)
    cp_b0 = to_sib(brow, first.at[low], i_send.at[2], i_recv.at[2])
    cp_b1 = to_sib(brow, O.at[high], i_send.at[2], i_recv.at[2])
    nxt = [
        remote(first.at[h], first.at[h], n_send.at[i], n_recv.at[i], s + 1, 0)
        for i, h in enumerate((low, high))
    ]
    fwd = [
        to_sib(first.at[h], O.at[h], f_send.at[i], f_recv.at[i]) for i, h in enumerate((low, high))
    ]

    @pl.when(c == 0)
    def _():
        cp_b0.start()
        O[0:H, :] = brow[...]

    @pl.when(c == 1)
    def _():
        cp_b1.start()
        first[H:N, :] = brow[...]

    cp_m.start()
    cp_r.start()

    @pl.when(c == 1)
    def _():
        cp_b0.wait_recv()

        @pl.when(s < slabs - 1)
        def _():
            nxt[0].start()
            nxt[1].start()

        @pl.when(s > 0)
        def _():
            fwd[0].wait_recv()
            fwd[1].wait_recv()

        @pl.when(s == 0)
        def _():
            O[...] = jnp.zeros((N, N), F32)

        cp_b1.wait_send()

    @pl.when(c == 0)
    def _():
        @pl.when(s > 0)
        def _():
            nxt[0].wait_recv()
            fwd[0].start()
            nxt[1].wait_recv()
            fwd[1].start()

        @pl.when(s == 0)
        def _():
            first[...] = jnp.zeros((N, N), F32)

        cp_b1.wait_recv()
        cp_b0.wait_send()

    cp_m.wait()
    mass = mrow[0:1, :] + mb[0:1, :]
    eye = lax.broadcasted_iota(jnp.int32, (T, T), 0) == lax.broadcasted_iota(jnp.int32, (T, T), 1)
    for n, (i, j) in enumerate(TILES):
        rr, cc = slice(T * i, T * i + T), slice(T * j, T * j + T)
        tile = first[rr, cc] + O[rr, cc]
        if i == j:
            tile = tile + jnp.where(eye, jnp.broadcast_to(mass[:, cc], (T, T)), 0.0)
        D[n] = tile
    cp_r.wait()

    @pl.when((c == 1) & (s < slabs - 1))
    def _():
        nxt[0].wait_send()
        nxt[1].wait_send()

    @pl.when((c == 0) & (s > 0))
    def _():
        fwd[0].wait_send()
        fwd[1].wait_send()

    @pl.when(jnp.logical_not(inside(s + sgn)))
    def _():
        first[...] = jnp.zeros((N, N), F32)

    T2[...] = jnp.zeros((2, H, H), F32)

    def step(k, d):
        prev = d // 2
        e = inside(s + sgn * d) & (k < levels)
        e_prev = inside(s + sgn * prev) & (k >= 1)
        e_sib = inside(s - sgn * prev) & (k >= 1)
        kp = jnp.maximum(k - 1, 0)
        peer = s + sgn * d
        peer_prev = s + sgn * prev

        def q_copy(p, level, to):
            o, n = PIECES[p]
            return remote(
                sendQ.at[pl.ds(o, n)],
                recvQ.at[level, pl.ds(o, n)],
                q_send.at[p],
                q_recv.at[level, p],
                to,
                sib,
            )

        def q_forward(p, level):
            o, n = PIECES[p]
            return to_sib(
                recvQ.at[level, pl.ds(o, n)],
                sibQ.at[level, pl.ds(o, n)],
                qf_send.at[p],
                qf_recv.at[level, p],
            )

        def p_copy(h, level, to):
            rows = pl.ds(pl.multiple_of(h * H, H), H)
            return remote(
                sendP.at[rows],
                recvP.at[level + 1, rows],
                p_send.at[h],
                p_recv.at[level, h],
                to,
                sib,
            )

        def v_copy(h, level):
            rows = pl.ds(pl.multiple_of(h * H, H), H)
            return to_sib(VX.at[rows], VY.at[level, rows], v_send.at[h], v_recv.at[level, h])

        def r_copy(level, to):
            return remote(sendR, recvR.at[level], r_send, r_recv.at[level], to, sib)

        def r_forward(level):
            return to_sib(recvR.at[level], sibR.at[level], rf_send, rf_recv.at[level])

        def take(p):
            o, n = PIECES[p]

            @pl.when(e_prev)
            def _():
                q_copy(p, kp, peer_prev).wait_recv()
                q_forward(p, kp).start()
                D[o : o + n] = D[o : o + n] - recvQ[kp, o : o + n]

            @pl.when(e_sib)
            def _():
                q_forward(p, kp).wait_recv()
                D[o : o + n] = D[o : o + n] - sibQ[kp, o : o + n]

            DW[o : o + n] = D[o : o + n]

            @pl.when(e_prev)
            def _():
                q_forward(p, kp).wait_send()

        take(0)

        def quarter(i, _):
            h = i // 2
            inv = leaf(DW[7 * h + 2 * (i - 2 * h)], scr)

            @pl.when(i == 2 * h)
            def _():
                T2[h, 0:T, 0:T] = inv
                g = dot(DW[7 * h + 1], inv)
                DW[7 * h + 2] = DW[7 * h + 2] - dot(g, g)
                W[...] = dot(g, inv, NN)

            @pl.when(i == 2 * h + 1)
            def _():
                T2[h, T:H, T:H] = inv
                T2[h, T:H, 0:T] = -dot(inv, W[...], NN)

            @pl.when(i == 1)
            def _():
                take(1)
                ba = jnp.concatenate(
                    [
                        jnp.concatenate([DW[3], DW[5]], 1),
                        jnp.concatenate([DW[4], DW[6]], 1),
                    ],
                    0,
                )
                g = dot(ba, T2[0])
                G[...] = g
                gg = dot(g, g)
                take(2)
                DW[7] = DW[7] - gg[0:T, 0:T]
                DW[8] = DW[8] - gg[T:H, 0:T]
                DW[9] = DW[9] - gg[T:H, T:H]

            return 0

        lax.fori_loop(0, 4, quarter, 0)

        @pl.when(k < levels)
        def _():
            def solve(h, _):
                rows = pl.ds(pl.multiple_of(h * H, H), H)

                @pl.when(e_prev)
                def _():
                    p_copy(h, kp, peer_prev).wait_recv()

                @pl.when((k >= 1))
                def _():
                    v_copy(h, kp).wait_send()

                va = dot(recvP[k, rows, 0:H], T2[0])
                VX[rows, 0:H] = va
                VX[rows, H:N] = dot(recvP[k, rows, H:N] - dot(va, G[...]), T2[1])

                @pl.when(k < levels - 1)
                def _():
                    v_copy(h, k).start()

                return 0

            lax.fori_loop(0, 2, solve, 0)

            for p, (i, j) in enumerate(((0, 0), (1, 0), (1, 1))):
                qq = dot(VX[i * H : i * H + H, :], VX[j * H : j * H + H, :])

                @pl.when(e_prev)
                def _():
                    q_copy(p, kp, peer_prev).wait_send()

                for n in range(PIECES[p][0], PIECES[p][0] + PIECES[p][1]):
                    r0, c0 = TILES[n][0] * T - i * H, TILES[n][1] * T - j * H
                    sendQ[n] = qq[r0 : r0 + T, c0 : c0 + T]

                @pl.when(e)
                def _():
                    q_copy(p, k, peer).start()

        @pl.when(k < levels - 1)
        def _():
            def product(h, _):
                rows = pl.ds(pl.multiple_of(h * H, H), H)
                v_copy(h, k).wait_recv()

                @pl.when(e_prev)
                def _():
                    p_copy(h, kp, peer_prev).wait_send()

                sendP[rows, :] = dot(VY[k, rows, :], VX[...])

                @pl.when(e)
                def _():
                    p_copy(h, k, peer).start()

                @pl.when(jnp.logical_not(e))
                def _():
                    recvP[k + 1, rows, :] = jnp.zeros((H, N), F32)

                return 0

            lax.fori_loop(0, 2, product, 0)

        @pl.when((k == levels - 1) & e_prev)
        def _():
            p_copy(0, kp, peer_prev).wait_send()
            p_copy(1, kp, peer_prev).wait_send()

        @pl.when(e_prev)
        def _():
            r_copy(kp, peer_prev).wait_recv()
            r_forward(kp).start()
            RT[...] = RT[...] + recvR[kp]

        @pl.when(e_sib)
        def _():
            r_forward(kp).wait_recv()
            RT[...] = RT[...] + sibR[kp]

        @pl.when(e_prev)
        def _():
            r_forward(kp).wait_send()
            r_copy(kp, peer_prev).wait_send()

        @pl.when(k < levels)
        def _():
            va = dot(RT[:, 0:H], T2[0])
            VR[:, 0:H] = va
            VR[:, H:N] = dot(RT[:, H:N] - dot(va, G[...]), T2[1])
            sendR[...] = dot(VR[...], VX[...])

            @pl.when(e)
            def _():
                r_copy(k, peer).start()

        @pl.when((k == levels) & e_prev)
        def _():
            for p in range(3):
                q_copy(p, kp, peer_prev).wait_send()

        return d * 2

    lax.fori_loop(0, levels + 1, step, 1)

    va = dot(RT[own_rt, 0:H], T2[0])
    vb = dot(RT[own_rt, H:N] - dot(va, G[...]), T2[1])
    xb = dot(vb, T2[1], NN)
    out[:, H:N] = xb
    out[:, 0:H] = dot(va - dot(xb, G[...], NN), T2[0], NN)


def solution(mesh):
    slabs = mesh.shape["slab"]
    levels = (slabs - 1).bit_length()

    def on_device(coupling, tile_pattern, orbital_mass, sources):
        column = lax.axis_index("col")
        pattern = tile_pattern[0]
        mask = jnp.broadcast_to(
            pattern.T[:, None, :, None].astype(F32), (N // T // 2, T, N // T, T)
        ).reshape(H, N)
        rows = lax.broadcasted_iota(jnp.int32, (H, N), 0) + column * H
        cols = lax.broadcasted_iota(jnp.int32, (H, N), 1)
        brow = (rows == cols).astype(F32) + mask * coupling[0].T
        both = jnp.concatenate([orbital_mass[0], orbital_mass[0]])
        mine = (jnp.arange(N) // H == column).astype(F32)
        mrow = jnp.broadcast_to((both * mine)[None], (8, N))
        dma = pltpu.SemaphoreType.DMA
        vmem = pl.BlockSpec(memory_space=pltpu.VMEM)
        xt = pl.pallas_call(
            functools.partial(kernel, slabs, levels),
            out_shape=jax.ShapeDtypeStruct((T, N), F32),
            in_specs=[vmem] * 3,
            out_specs=vmem,
            scratch_shapes=[
                pltpu.VMEM((levels, N, N), F32),
                pltpu.VMEM((levels, 10, T, T), F32),
                pltpu.VMEM((levels, 10, T, T), F32),
                pltpu.VMEM((levels, M, N), F32),
                pltpu.VMEM((levels, M, N), F32),
                pltpu.VMEM((levels, N, N), F32),
                pltpu.VMEM((N, N), F32),
                pltpu.VMEM((N, N), F32),
                pltpu.VMEM((M, N), F32),
                pltpu.VMEM((M, N), F32),
                pltpu.VMEM((10, T, T), F32),
                pltpu.VMEM((10, T, T), F32),
                pltpu.VMEM((2, H, H), F32),
                pltpu.VMEM((H, H), F32),
                pltpu.VMEM((T, T), F32),
                pltpu.VMEM((18, 8, T), F32),
                pltpu.VMEM((8, N), F32),
                pltpu.VMEM((10, T, T), F32),
                pltpu.VMEM((N, N), F32),
                pltpu.VMEM((M, N), F32),
                dma((3,)),
                dma((3,)),
                dma((2,)),
                dma((2,)),
                dma((2,)),
                dma((2,)),
                dma((2,)),
                dma((levels, 2)),
                dma((3,)),
                dma((levels, 3)),
                dma((3,)),
                dma((levels, 3)),
                dma((2,)),
                dma((levels, 2)),
                dma(()),
                dma((levels,)),
                dma(()),
                dma((levels,)),
            ],
            compiler_params=pltpu.CompilerParams(
                collective_id=0, has_side_effects=True, vmem_limit_bytes=56 << 20
            ),
        )(brow, sources[0].T, mrow)
        return xt.T[None]

    placed = (
        P("slab", None, "col"),
        P("slab", None, "col"),
        P("slab", "col"),
        P("slab", None, "col"),
    )
    return jax.shard_map(
        on_device, mesh=mesh, in_specs=placed, out_specs=P("slab", None, "col"), check_vma=False
    )
```

time: 1250 us -> 259 us (0.21)
  other arithmetic: 694 us -> 1.67 us
  waiting for transfers between devices: 314 us -> 0 us
  Pallas kernels: 0 us -> 251 us
  matrix products: 142 us -> 0 us
  starting transfers between devices: 40.7 us -> 0 us
  local copies, waits for them, and re-layouts: 34.1 us -> 4.41 us
  between operations: 16.6 us -> 0.04 us
    another operation x140 -> x0, other arithmetic: 660 us -> none  [the longest x84 363 us: factor_inverse(): factor = jnp.linalg.cholesky(matrix)]
    pallas_call x0 -> x1, Pallas kernels: none -> 251 us  [on_device(): pl.pallas_call(functools.partial(kernel, slabs, levels), out_shape=jax.Sh...]
    ppermute x13 -> x0, waiting for transfers between devices: 222 us -> none  [from_behind(): return lax.ppermute(shard, axis, pairs)]
    dot_general x110 -> x0, matrix products: 134 us -> none  [the longest x6 25.6 us: on_device(): jnp.dot(full_upper, from_above, precision=lax.Precision.HIGHEST, preferre...]
    all_gather x19 -> x0, waiting for transfers between devices: 90.7 us -> none  [the longest x6 77.5 us: on_device(): lax.all_gather(diag_panel, 'col', axis=1, tiled=True)]
    ppermute x13 -> x0, starting transfers between devices: 38 us -> none  [from_behind(): return lax.ppermute(shard, axis, pairs)]
    unnamed x90 -> x8, local copies, waits for them, and re-layouts: 19.2 us -> 1.89 us
  transfers between devices with their start and end apart: 32 -> 0, of which waited for: 18 -> 0; matrix products, arithmetic and copies ran while one was open for 56% -> 0% of each run, Pallas kernels for 0% -> 0%
where the time goes in v1:
time: 259 us; the launch traced here: 257 us
  Pallas kernels  251 us (97%)
  local copies, waits for them, and re-layouts  4.41 us (2%)
    pallas_call x1, Pallas kernels, on_device(): pl.pallas_call(functools.partial(kernel, slabs, levels), out_shape=jax.Sh...  251 us

profile of v1, /device:TPU:31, one launch (start us, length us, event | category | flops | bytes accessed | tf_op | source)
XLA Modules:
  0.0 257.0 jit_solution(15587984039858025257)
XLA Ops:
  0.0 0.0 copy-start
  0.0 0.7 convert_bitcast_fusion
  0.7 0.1 broadcast_in_dim.6
  0.9 0.2 copy-done
  1.1 0.2 copy.5
  1.3 0.0 copy-start.1
  1.3 0.9 fusion.brow
  2.2 0.0 copy-start.2
  2.2 0.7 copy-done.2
  2.9 0.6 broadcast_in_dim.7.mrow
  3.5 0.0 copy-done.1
  3.5 0.8 copy.6
  4.3 250.9 %shard_map.46 = f32[128,512]{1,0:T(8,128)} custom-call(f32[256,512]{1,0:T(8,128)} %fusion.brow, f32[128,512]{1,0:T(8,128)} %bitcast.23, f32[8,512]{1,0:T(8,128)} %broadcast_in_dim.7.mrow), custom_call_target="tpu_custom_call" | custom-call | tf_op jit(solution)/shard_map/pallas_call | solution.py:495
  255.2 1.8 copy.7
  (2 shorter events, 0.0 us)
Async XLA Ops:
  0.0 1.1 copy-start
  1.3 2.2 copy-start.1
  2.2 0.7 copy-start.2

commit v2 on v1

--- a/solution.py
+++ b/solution.py
@@ -15,7 +15,7 @@
 NT = (((1,), (1,)), ((), ()))
 NN = (((1,), (0,)), ((), ()))
 TILES = ((0, 0), (1, 0), (1, 1), (2, 0), (3, 0), (2, 1), (3, 1), (2, 2), (3, 2), (3, 3))
-PIECES = ((0, 3), (3, 4), (7, 3))
+PIECES = ((0, 1), (1, 2), (3, 4), (7, 3))
 MESH = pl.DeviceIdType.MESH
 
 
@@ -165,90 +165,92 @@
     to_sib = functools.partial(remote, slab=s, col=sib)
     cp_m = to_sib(mrow, mb, i_send.at[0], i_recv.at[0])
     cp_r = to_sib(srct, RT.at[own_rt], i_send.at[1], i_recv.at[1])
-    low, high = pl.ds(0, H), pl.ds(H, H)
+    low, high, full = pl.ds(0, H), pl.ds(H, H), pl.ds(0, N)
     cp_b0 = to_sib(brow, first.at[low], i_send.at[2], i_recv.at[2])
     cp_b1 = to_sib(brow, O.at[high], i_send.at[2], i_recv.at[2])
+    parts = ((low, low), (high, full), (low, high))
     nxt = [
-        remote(first.at[h], first.at[h], n_send.at[i], n_recv.at[i], s + 1, 0)
-        for i, h in enumerate((low, high))
+        remote(first.at[p], first.at[p], n_send.at[i], n_recv.at[i], s + 1, 0)
+        for i, p in enumerate(parts)
     ]
-    fwd = [
-        to_sib(first.at[h], O.at[h], f_send.at[i], f_recv.at[i]) for i, h in enumerate((low, high))
-    ]
+    fwd = [to_sib(first.at[p], O.at[p], f_send.at[i], f_recv.at[i]) for i, p in enumerate(parts[:2])]
+    has_next, has_prior = s < slabs - 1, s > 0
 
     @pl.when(c == 0)
     def _():
         cp_b0.start()
         O[0:H, :] = brow[...]
 
+        @pl.when(s == 0)
+        def _():
+            first[...] = jnp.zeros((N, N), F32)
+
     @pl.when(c == 1)
     def _():
         cp_b1.start()
         first[H:N, :] = brow[...]
+        cp_b0.wait_recv()
+
+        @pl.when(has_next)
+        def _():
+            for copy in nxt:
+                copy.start()
+
+        @pl.when(s == 0)
+        def _():
+            O[...] = jnp.zeros((N, N), F32)
 
     cp_m.start()
     cp_r.start()
+    cp_m.wait()
+    cp_r.wait()
+
+    @pl.when(c == 0)
+    def _():
+        cp_b1.wait_recv()
+        cp_b0.wait_send()
 
     @pl.when(c == 1)
     def _():
-        cp_b0.wait_recv()
-
-        @pl.when(s < slabs - 1)
-        def _():
-            nxt[0].start()
-            nxt[1].start()
-
-        @pl.when(s > 0)
-        def _():
-            fwd[0].wait_recv()
-            fwd[1].wait_recv()
-
-        @pl.when(s == 0)
-        def _():
-            O[...] = jnp.zeros((N, N), F32)
-
         cp_b1.wait_send()
 
-    @pl.when(c == 0)
-    def _():
-        @pl.when(s > 0)
-        def _():
-            nxt[0].wait_recv()
-            fwd[0].start()
-            nxt[1].wait_recv()
-            fwd[1].start()
-
-        @pl.when(s == 0)
+    def arrive(part):
+        @pl.when((c == 0) & has_prior)
+        def _():
+            nxt[part].wait_recv()
+            fwd[part].start()
+
+        @pl.when((c == 1) & has_prior)
+        def _():
+            fwd[part].wait_recv()
+
+    eye = lax.broadcasted_iota(jnp.int32, (T, T), 0) == lax.broadcasted_iota(jnp.int32, (T, T), 1)
+
+    def build(p):
+        for n in range(PIECES[p][0], PIECES[p][0] + PIECES[p][1]):
+            i, j = TILES[n]
+            rr, cc = slice(T * i, T * i + T), slice(T * j, T * j + T)
+            tile = first[rr, cc] + O[rr, cc]
+            if i == j:
+                mass = mrow[0:1, cc] + mb[0:1, cc]
+                tile = tile + jnp.where(eye, jnp.broadcast_to(mass, (T, T)), 0.0)
+            D[n] = tile
+
+    def finish_first():
+        @pl.when((c == 0) & has_prior)
+        def _():
+            nxt[2].wait_recv()
+            fwd[0].wait_send()
+            fwd[1].wait_send()
+
+        @pl.when((c == 1) & has_next)
+        def _():
+            for copy in nxt:
+                copy.wait_send()
+
+        @pl.when((c == 1) & jnp.logical_not(has_next))
         def _():
             first[...] = jnp.zeros((N, N), F32)
-
-        cp_b1.wait_recv()
-        cp_b0.wait_send()
-
-    cp_m.wait()
-    mass = mrow[0:1, :] + mb[0:1, :]
-    eye = lax.broadcasted_iota(jnp.int32, (T, T), 0) == lax.broadcasted_iota(jnp.int32, (T, T), 1)
-    for n, (i, j) in enumerate(TILES):
-        rr, cc = slice(T * i, T * i + T), slice(T * j, T * j + T)
-        tile = first[rr, cc] + O[rr, cc]
-        if i == j:
-            tile = tile + jnp.where(eye, jnp.broadcast_to(mass[:, cc], (T, T)), 0.0)
-        D[n] = tile
-    cp_r.wait()
-
-    @pl.when((c == 1) & (s < slabs - 1))
-    def _():
-        nxt[0].wait_send()
-        nxt[1].wait_send()
-
-    @pl.when((c == 0) & (s > 0))
-    def _():
-        fwd[0].wait_send()
-        fwd[1].wait_send()
-
-    @pl.when(jnp.logical_not(inside(s + sgn)))
-    def _():
-        first[...] = jnp.zeros((N, N), F32)
 
     T2[...] = jnp.zeros((2, H, H), F32)
 
@@ -305,6 +307,12 @@
         def take(p):
             o, n = PIECES[p]
 
+            @pl.when(k == 0)
+            def _():
+                if p in (0, 2):
+                    arrive(p // 2)
+                build(p)
+
             @pl.when(e_prev)
             def _():
                 q_copy(p, kp, peer_prev).wait_recv()
@@ -327,6 +335,10 @@
         def quarter(i, _):
             h = i // 2
             inv = leaf(DW[7 * h + 2 * (i - 2 * h)], scr)
+
+            @pl.when(i == 0)
+            def _():
+                take(1)
 
             @pl.when(i == 2 * h)
             def _():
@@ -342,7 +354,7 @@
 
             @pl.when(i == 1)
             def _():
-                take(1)
+                take(2)
                 ba = jnp.concatenate(
                     [
                         jnp.concatenate([DW[3], DW[5]], 1),
@@ -353,7 +365,7 @@
                 g = dot(ba, T2[0])
                 G[...] = g
                 gg = dot(g, g)
-                take(2)
+                take(3)
                 DW[7] = DW[7] - gg[0:T, 0:T]
                 DW[8] = DW[8] - gg[T:H, 0:T]
                 DW[9] = DW[9] - gg[T:H, T:H]
@@ -364,14 +376,18 @@
 
         @pl.when(k < levels)
         def _():
-            def solve(h, _):
-                rows = pl.ds(pl.multiple_of(h * H, H), H)
+            @pl.when(k == 0)
+            def _():
+                finish_first()
+
+            def solve(h):
+                rows = slice(h * H, h * H + H)
 
                 @pl.when(e_prev)
                 def _():
                     p_copy(h, kp, peer_prev).wait_recv()
 
-                @pl.when((k >= 1))
+                @pl.when(k >= 1)
                 def _():
                     v_copy(h, kp).wait_send()
 
@@ -383,24 +399,27 @@
                 def _():
                     v_copy(h, k).start()
 
-                return 0
-
-            lax.fori_loop(0, 2, solve, 0)
-
-            for p, (i, j) in enumerate(((0, 0), (1, 0), (1, 1))):
+            def diagonal(i, j, pieces):
                 qq = dot(VX[i * H : i * H + H, :], VX[j * H : j * H + H, :])
-
-                @pl.when(e_prev)
-                def _():
-                    q_copy(p, kp, peer_prev).wait_send()
-
-                for n in range(PIECES[p][0], PIECES[p][0] + PIECES[p][1]):
-                    r0, c0 = TILES[n][0] * T - i * H, TILES[n][1] * T - j * H
-                    sendQ[n] = qq[r0 : r0 + T, c0 : c0 + T]
-
-                @pl.when(e)
-                def _():
-                    q_copy(p, k, peer).start()
+                for p in pieces:
+
+                    @pl.when(e_prev)
+                    def _():
+                        q_copy(p, kp, peer_prev).wait_send()
+
+                    for n in range(PIECES[p][0], PIECES[p][0] + PIECES[p][1]):
+                        r0, c0 = TILES[n][0] * T - i * H, TILES[n][1] * T - j * H
+                        sendQ[n] = qq[r0 : r0 + T, c0 : c0 + T]
+
+                    @pl.when(e)
+                    def _():
+                        q_copy(p, k, peer).start()
+
+            solve(0)
+            diagonal(0, 0, (0, 1))
+            solve(1)
+            diagonal(1, 0, (2,))
+            diagonal(1, 1, (3,))
 
         @pl.when(k < levels - 1)
         def _():
@@ -460,7 +479,7 @@
 
         @pl.when((k == levels) & e_prev)
         def _():
-            for p in range(3):
+            for p in range(len(PIECES)):
                 q_copy(p, kp, peer_prev).wait_send()
 
         return d * 2
@@ -520,16 +539,16 @@
                 pltpu.VMEM((M, N), F32),
                 dma((3,)),
                 dma((3,)),
-                dma((2,)),
-                dma((2,)),
+                dma((3,)),
+                dma((3,)),
                 dma((2,)),
                 dma((2,)),
                 dma((2,)),
                 dma((levels, 2)),
-                dma((3,)),
-                dma((levels, 3)),
-                dma((3,)),
-                dma((levels, 3)),
+                dma((len(PIECES),)),
+                dma((levels, len(PIECES))),
+                dma((len(PIECES),)),
+                dma((levels, len(PIECES))),
                 dma((2,)),
                 dma((levels, 2)),
                 dma(()),

time: 259 us -> 254 us (0.981)
  Pallas kernels: 251 us -> 245 us
    pallas_call x1, Pallas kernels: 251 us -> 245 us  [on_device(): pl.pallas_call(functools.partial(kernel, slabs, levels), out_shape=jax.Sh...]
where the time goes in v2:
time: 254 us; the launch traced here: 251 us
  Pallas kernels  245 us (96%)
  local copies, waits for them, and re-layouts  4.41 us (2%)
    pallas_call x1, Pallas kernels, on_device(): pl.pallas_call(functools.partial(kernel, slabs, levels), out_shape=jax.Sh...  245 us

profile of v2, /device:TPU:31, one launch (start us, length us, event | category | flops | bytes accessed | tf_op | source)
XLA Modules:
  0.0 250.7 jit_solution(15194695977030028090)
XLA Ops:
  0.0 0.0 copy-start
  0.0 0.7 convert_bitcast_fusion
  0.7 0.1 broadcast_in_dim.6
  0.9 0.2 copy-done
  1.1 0.2 copy.5
  1.3 0.0 copy-start.1
  1.3 0.9 fusion.brow
  2.2 0.0 copy-start.2
  2.2 0.7 copy-done.2
  2.9 0.6 broadcast_in_dim.7.mrow
  3.5 0.0 copy-done.1
  3.5 0.8 copy.6
  4.3 244.5 %shard_map.46 = f32[128,512]{1,0:T(8,128)} custom-call(f32[256,512]{1,0:T(8,128)} %fusion.brow, f32[128,512]{1,0:T(8,128)} %bitcast.23, f32[8,512]{1,0:T(8,128)} %broadcast_in_dim.7.mrow), custom_call_target="tpu_custom_call" | custom-call | tf_op jit(solution)/shard_map/pallas_call | solution.py:514
  248.9 1.8 copy.7
  (2 shorter events, 0.0 us)
Async XLA Ops:
  0.0 1.1 copy-start
  1.3 2.2 copy-start.1
  2.2 0.7 copy-start.2

commit v3 on v2

--- a/solution.py
+++ b/solution.py
@@ -106,6 +106,8 @@
     sendQ,
     sendP,
     sendR,
+    xrecv,
+    xsum,
     i_send,
     i_recv,
     n_send,
@@ -124,14 +126,28 @@
     r_recv,
     rf_send,
     rf_recv,
+    x_send,
+    x_recv,
 ):
     s = lax.axis_index("slab")
     c = lax.axis_index("col")
     sgn = 2 * c - 1
     sib = 1 - c
 
+    eliminating = tuple(range(1, levels - 1, 2))
+
     def inside(t):
         return (t >= 0) & (t < slabs)
+
+    def eliminates(k):
+        return (k % 2 == 1) & (k < levels - 1)
+
+    def odd(t, d):
+        return ((t + slabs) // d) % 2 == 1
+
+    own_level = levels
+    for k in reversed(eliminating):
+        own_level = jnp.where(odd(s, 2**k), k, own_level)
 
     def remote(src, dst, ss, rs, slab, col):
         return pltpu.make_async_remote_copy(
@@ -156,6 +172,17 @@
             pl.semaphore_signal(
                 barrier, inc=1, device_id={"slab": peer, "col": sib}, device_id_type=MESH
             )
+
+    for k in eliminating:
+        for peer in (s - 2**k, s + 2**k):
+            here = inside(peer)
+            count = count + here.astype(jnp.int32)
+
+            @pl.when(here)
+            def _():
+                pl.semaphore_signal(
+                    barrier, inc=1, device_id={"slab": peer, "col": c}, device_id_type=MESH
+                )
 
     pl.semaphore_wait(barrier, count)
 
@@ -256,12 +283,20 @@
 
     def step(k, d):
         prev = d // 2
-        e = inside(s + sgn * d) & (k < levels)
-        e_prev = inside(s + sgn * prev) & (k >= 1)
-        e_sib = inside(s - sgn * prev) & (k >= 1)
         kp = jnp.maximum(k - 1, 0)
         peer = s + sgn * d
         peer_prev = s + sgn * prev
+        alive = k <= own_level
+        work = alive & jnp.logical_not(eliminates(k) & (own_level != k))
+        work_prev = (k >= 1) & (kp <= own_level) & jnp.logical_not(eliminates(kp) & (own_level != kp))
+        rx = (k >= 1) & alive & inside(peer_prev)
+        rx_sib = (k >= 1) & alive & inside(s - sgn * prev)
+        rx_p = rx & (k < levels) & (jnp.logical_not(eliminates(k)) | (own_level == k))
+        tx = work & (k < levels) & inside(peer)
+        tx_p = tx & (k < levels - 1) & (jnp.logical_not(eliminates(k + 1)) | odd(peer, 2 * d))
+        tx_prev = work_prev & inside(peer_prev)
+        tx_p_prev = tx_prev & (k < levels) & (jnp.logical_not(eliminates(k)) | odd(peer_prev, d))
+        tx_v_prev = work_prev & (k < levels)
 
         def q_copy(p, level, to):
             o, n = PIECES[p]
@@ -304,6 +339,26 @@
         def r_forward(level):
             return to_sib(recvR.at[level], sibR.at[level], rf_send, rf_recv.at[level])
 
+        def sent_q(p):
+            @pl.when(tx_prev)
+            def _():
+                q_copy(p, kp, peer_prev).wait_send()
+
+        def sent_p(h):
+            @pl.when(tx_p_prev)
+            def _():
+                p_copy(h, kp, peer_prev).wait_send()
+
+        def sent_v(h):
+            @pl.when(tx_v_prev)
+            def _():
+                v_copy(h, kp).wait_send()
+
+        def sent_r():
+            @pl.when(tx_prev)
+            def _():
+                r_copy(kp, peer_prev).wait_send()
+
         def take(p):
             o, n = PIECES[p]
 
@@ -313,24 +368,22 @@
                     arrive(p // 2)
                 build(p)
 
-            @pl.when(e_prev)
+            @pl.when(rx)
             def _():
                 q_copy(p, kp, peer_prev).wait_recv()
                 q_forward(p, kp).start()
                 D[o : o + n] = D[o : o + n] - recvQ[kp, o : o + n]
 
-            @pl.when(e_sib)
+            @pl.when(rx_sib)
             def _():
                 q_forward(p, kp).wait_recv()
                 D[o : o + n] = D[o : o + n] - sibQ[kp, o : o + n]
 
             DW[o : o + n] = D[o : o + n]
 
-            @pl.when(e_prev)
+            @pl.when(rx)
             def _():
                 q_forward(p, kp).wait_send()
-
-        take(0)
 
         def quarter(i, _):
             h = i // 2
@@ -372,25 +425,34 @@
 
             return 0
 
-        lax.fori_loop(0, 4, quarter, 0)
-
-        @pl.when(k < levels)
+        @pl.when(work)
+        def _():
+            take(0)
+            lax.fori_loop(0, 4, quarter, 0)
+
+        @pl.when(alive & jnp.logical_not(work))
+        def _():
+            for p in range(len(PIECES)):
+                take(p)
+
+        @pl.when(work & (k < levels))
         def _():
             @pl.when(k == 0)
             def _():
                 finish_first()
+
+            @pl.when((k >= 1) & jnp.logical_not(inside(peer_prev)))
+            def _():
+                recvP[k] = jnp.zeros((N, N), F32)
 
             def solve(h):
                 rows = slice(h * H, h * H + H)
 
-                @pl.when(e_prev)
+                @pl.when(rx_p)
                 def _():
                     p_copy(h, kp, peer_prev).wait_recv()
 
-                @pl.when(k >= 1)
-                def _():
-                    v_copy(h, kp).wait_send()
-
+                sent_v(h)
                 va = dot(recvP[k, rows, 0:H], T2[0])
                 VX[rows, 0:H] = va
                 VX[rows, H:N] = dot(recvP[k, rows, H:N] - dot(va, G[...]), T2[1])
@@ -402,16 +464,12 @@
             def diagonal(i, j, pieces):
                 qq = dot(VX[i * H : i * H + H, :], VX[j * H : j * H + H, :])
                 for p in pieces:
-
-                    @pl.when(e_prev)
-                    def _():
-                        q_copy(p, kp, peer_prev).wait_send()
-
+                    sent_q(p)
                     for n in range(PIECES[p][0], PIECES[p][0] + PIECES[p][1]):
                         r0, c0 = TILES[n][0] * T - i * H, TILES[n][1] * T - j * H
                         sendQ[n] = qq[r0 : r0 + T, c0 : c0 + T]
 
-                    @pl.when(e)
+                    @pl.when(tx)
                     def _():
                         q_copy(p, k, peer).start()
 
@@ -421,76 +479,112 @@
             diagonal(1, 0, (2,))
             diagonal(1, 1, (3,))
 
-        @pl.when(k < levels - 1)
-        def _():
             def product(h, _):
                 rows = pl.ds(pl.multiple_of(h * H, H), H)
-                v_copy(h, k).wait_recv()
-
-                @pl.when(e_prev)
+                sent_p(h)
+
+                @pl.when(k < levels - 1)
                 def _():
-                    p_copy(h, kp, peer_prev).wait_send()
-
-                sendP[rows, :] = dot(VY[k, rows, :], VX[...])
-
-                @pl.when(e)
+                    v_copy(h, k).wait_recv()
+
+                @pl.when(tx_p)
                 def _():
+                    sendP[rows, :] = dot(VY[k, rows, :], VX[...])
                     p_copy(h, k, peer).start()
 
-                @pl.when(jnp.logical_not(e))
-                def _():
-                    recvP[k + 1, rows, :] = jnp.zeros((H, N), F32)
-
                 return 0
 
             lax.fori_loop(0, 2, product, 0)
 
-        @pl.when((k == levels - 1) & e_prev)
-        def _():
-            p_copy(0, kp, peer_prev).wait_send()
-            p_copy(1, kp, peer_prev).wait_send()
-
-        @pl.when(e_prev)
+        @pl.when(rx)
         def _():
             r_copy(kp, peer_prev).wait_recv()
             r_forward(kp).start()
             RT[...] = RT[...] + recvR[kp]
 
-        @pl.when(e_sib)
+        @pl.when(rx_sib)
         def _():
             r_forward(kp).wait_recv()
             RT[...] = RT[...] + sibR[kp]
 
-        @pl.when(e_prev)
+        @pl.when(rx)
         def _():
             r_forward(kp).wait_send()
-            r_copy(kp, peer_prev).wait_send()
-
-        @pl.when(k < levels)
+
+        sent_r()
+
+        @pl.when(work & (k < levels))
         def _():
             va = dot(RT[:, 0:H], T2[0])
             VR[:, 0:H] = va
             VR[:, H:N] = dot(RT[:, H:N] - dot(va, G[...]), T2[1])
             sendR[...] = dot(VR[...], VX[...])
 
-            @pl.when(e)
+            @pl.when(tx)
             def _():
                 r_copy(k, peer).start()
 
-        @pl.when((k == levels) & e_prev)
+        @pl.when(jnp.logical_not(work & (k < levels)))
         def _():
             for p in range(len(PIECES)):
-                q_copy(p, kp, peer_prev).wait_send()
+                sent_q(p)
+            for h in range(2):
+                sent_p(h)
+                sent_v(h)
 
         return d * 2
 
     lax.fori_loop(0, levels + 1, step, 1)
 
-    va = dot(RT[own_rt, 0:H], T2[0])
-    vb = dot(RT[own_rt, H:N] - dot(va, G[...]), T2[1])
-    xb = dot(vb, T2[1], NN)
-    out[:, H:N] = xb
-    out[:, 0:H] = dot(va - dot(xb, G[...], NN), T2[0], NN)
+    def backward(va, vb):
+        xb = dot(vb, T2[1], NN)
+        out[:, H:N] = xb
+        out[:, 0:H] = dot(va - dot(xb, G[...], NN), T2[0], NN)
+
+    @pl.when(own_level == levels)
+    def _():
+        va = dot(RT[own_rt, 0:H], T2[0])
+        backward(va, dot(RT[own_rt, H:N] - dot(va, G[...]), T2[1]))
+
+    for n, k in enumerate(reversed(eliminating)):
+        d = 2**k
+        ways = (s - sgn * d, s + sgn * d)
+
+        def x_copy(way):
+            return remote(out, xrecv.at[way], x_send.at[n, way], x_recv.at[way], ways[way], c)
+
+        for way in range(2):
+
+            @pl.when((own_level > k) & inside(ways[way]))
+            def _():
+                x_copy(way).start()
+
+        @pl.when(own_level == k)
+        def _():
+            xsum[...] = VR[own_rt, :]
+
+            @pl.when(inside(ways[1]))
+            def _():
+                x_copy(0).wait_recv()
+                xsum[...] = xsum[...] + dot(xrecv[0], VX[...], NN)
+
+            @pl.when(inside(ways[0]))
+            def _():
+                x_copy(1).wait_recv()
+                xsum[...] = xsum[...] + dot(xrecv[1], VY[k], NN)
+
+            backward(xsum[:, 0:H], xsum[:, H:N])
+
+    for n, k in enumerate(reversed(eliminating)):
+        d = 2**k
+        ways = (s - sgn * d, s + sgn * d)
+        for way in range(2):
+
+            @pl.when((own_level > k) & inside(ways[way]))
+            def _():
+                remote(
+                    out, xrecv.at[way], x_send.at[n, way], x_recv.at[way], ways[way], c
+                ).wait_send()
 
 
 def solution(mesh):
@@ -537,6 +631,8 @@
                 pltpu.VMEM((10, T, T), F32),
                 pltpu.VMEM((N, N), F32),
                 pltpu.VMEM((M, N), F32),
+                pltpu.VMEM((2, T, N), F32),
+                pltpu.VMEM((T, N), F32),
                 dma((3,)),
                 dma((3,)),
                 dma((3,)),
@@ -555,6 +651,8 @@
                 dma((levels,)),
                 dma(()),
                 dma((levels,)),
+                dma((levels, 2)),
+                dma((2,)),
             ],
             compiler_params=pltpu.CompilerParams(
                 collective_id=0, has_side_effects=True, vmem_limit_bytes=56 << 20

time: 254 us -> 283 us (1.11)
  the two profiles are of different devices: /device:TPU:31 before, /device:TPU:76 now
where the time goes in v3:
time: 283 us
  Pallas kernels  276 us (98%)
  local copies, waits for them, and re-layouts  4.41 us (2%)
    pallas_call x1, Pallas kernels, on_device(): pl.pallas_call(functools.partial(kernel, slabs, levels), out_shape=jax.Sh...  276 us

profile of v3, /device:TPU:76, one launch (start us, length us, event | category | flops | bytes accessed | tf_op | source)
XLA Modules:
  0.0 282.5 jit_solution(239103492376594549)
XLA Ops:
  0.0 0.0 copy-start
  0.0 0.7 convert_bitcast_fusion
  0.7 0.1 broadcast_in_dim.6
  0.9 0.2 copy-done
  1.1 0.2 copy.5
  1.3 0.0 copy-start.1
  1.3 0.9 fusion.brow
  2.2 0.0 copy-start.2
  2.2 0.7 copy-done.2
  2.9 0.6 broadcast_in_dim.7.mrow
  3.5 0.0 copy-done.1
  3.5 0.8 copy.6
  4.3 276.4 %shard_map.46 = f32[128,512]{1,0:T(8,128)} custom-call(f32[256,512]{1,0:T(8,128)} %fusion.brow, f32[128,512]{1,0:T(8,128)} %bitcast.23, f32[8,512]{1,0:T(8,128)} %broadcast_in_dim.7.mrow), custom_call_target="tpu_custom_call" | custom-call | tf_op jit(solution)/shard_map/pallas_call | solution.py:608
  280.7 1.8 copy.7
  (2 shorter events, 0.0 us)
Async XLA Ops:
  0.0 1.1 copy-start
  1.3 2.2 copy-start.1
  2.2 0.7 copy-start.2

commit v4 on v2

--- a/solution.py
+++ b/solution.py
@@ -83,7 +83,7 @@
     slabs,
     levels,
     brow,
-    srct,
+    src,
     mrow,
     out,
     recvP,
@@ -161,10 +161,10 @@
 
     first = recvP.at[0]
     own_rt = pl.ds(pl.multiple_of(c * T, T), T)
-    RT[own_rt, :] = srct[...]
+    RT[own_rt, :] = src[...].T
     to_sib = functools.partial(remote, slab=s, col=sib)
     cp_m = to_sib(mrow, mb, i_send.at[0], i_recv.at[0])
-    cp_r = to_sib(srct, RT.at[own_rt], i_send.at[1], i_recv.at[1])
+    cp_r = to_sib(RT.at[own_rt], RT.at[own_rt], i_send.at[1], i_recv.at[1])
     low, high, full = pl.ds(0, H), pl.ds(H, H), pl.ds(0, N)
     cp_b0 = to_sib(brow, first.at[low], i_send.at[2], i_recv.at[2])
     cp_b1 = to_sib(brow, O.at[high], i_send.at[2], i_recv.at[2])
@@ -252,10 +252,11 @@
         def _():
             first[...] = jnp.zeros((N, N), F32)
 
-    T2[...] = jnp.zeros((2, H, H), F32)
+    T2[...] = jnp.zeros((2, 2, H, H), F32)
 
     def step(k, d):
         prev = d // 2
+        slot, was = k % 2, (k + 1) % 2
         e = inside(s + sgn * d) & (k < levels)
         e_prev = inside(s + sgn * prev) & (k >= 1)
         e_sib = inside(s - sgn * prev) & (k >= 1)
@@ -332,6 +333,39 @@
 
         take(0)
 
+        def take_rhs(level, stride, on):
+            there = s + sgn * stride
+
+            @pl.when(on & inside(there))
+            def _():
+                r_copy(level, there).wait_recv()
+                r_forward(level).start()
+                RT[...] = RT[...] + recvR[level]
+
+            @pl.when(on & inside(s - sgn * stride))
+            def _():
+                r_forward(level).wait_recv()
+                RT[...] = RT[...] + sibR[level]
+
+            @pl.when(on & inside(there))
+            def _():
+                r_forward(level).wait_send()
+                r_copy(level, there).wait_send()
+
+        def rhs():
+            take_rhs(jnp.maximum(k - 2, 0), d // 4, k >= 2)
+
+            @pl.when(k >= 1)
+            def _():
+                va = dot(RT[:, 0:H], T2[was, 0])
+                VR[:, 0:H] = va
+                VR[:, H:N] = dot(RT[:, H:N] - dot(va, G[was]), T2[was, 1])
+                sendR[...] = dot(VR[...], VX[...])
+
+                @pl.when(e_prev)
+                def _():
+                    r_copy(kp, peer_prev).start()
+
         def quarter(i, _):
             h = i // 2
             inv = leaf(DW[7 * h + 2 * (i - 2 * h)], scr)
@@ -342,15 +376,15 @@
 
             @pl.when(i == 2 * h)
             def _():
-                T2[h, 0:T, 0:T] = inv
+                T2[slot, h, 0:T, 0:T] = inv
                 g = dot(DW[7 * h + 1], inv)
                 DW[7 * h + 2] = DW[7 * h + 2] - dot(g, g)
                 W[...] = dot(g, inv, NN)
 
             @pl.when(i == 2 * h + 1)
             def _():
-                T2[h, T:H, T:H] = inv
-                T2[h, T:H, 0:T] = -dot(inv, W[...], NN)
+                T2[slot, h, T:H, T:H] = inv
+                T2[slot, h, T:H, 0:T] = -dot(inv, W[...], NN)
 
             @pl.when(i == 1)
             def _():
@@ -362,13 +396,14 @@
                     ],
                     0,
                 )
-                g = dot(ba, T2[0])
-                G[...] = g
+                g = dot(ba, T2[slot, 0])
+                G[slot] = g
                 gg = dot(g, g)
                 take(3)
                 DW[7] = DW[7] - gg[0:T, 0:T]
                 DW[8] = DW[8] - gg[T:H, 0:T]
                 DW[9] = DW[9] - gg[T:H, T:H]
+                rhs()
 
             return 0
 
@@ -391,9 +426,9 @@
                 def _():
                     v_copy(h, kp).wait_send()
 
-                va = dot(recvP[k, rows, 0:H], T2[0])
+                va = dot(recvP[k, rows, 0:H], T2[slot, 0])
                 VX[rows, 0:H] = va
-                VX[rows, H:N] = dot(recvP[k, rows, H:N] - dot(va, G[...]), T2[1])
+                VX[rows, H:N] = dot(recvP[k, rows, H:N] - dot(va, G[slot]), T2[slot, 1])
 
                 @pl.when(k < levels - 1)
                 def _():
@@ -450,32 +485,9 @@
             p_copy(0, kp, peer_prev).wait_send()
             p_copy(1, kp, peer_prev).wait_send()
 
-        @pl.when(e_prev)
-        def _():
-            r_copy(kp, peer_prev).wait_recv()
-            r_forward(kp).start()
-            RT[...] = RT[...] + recvR[kp]
-
-        @pl.when(e_sib)
-        def _():
-            r_forward(kp).wait_recv()
-            RT[...] = RT[...] + sibR[kp]
-
-        @pl.when(e_prev)
-        def _():
-            r_forward(kp).wait_send()
-            r_copy(kp, peer_prev).wait_send()
-
-        @pl.when(k < levels)
-        def _():
-            va = dot(RT[:, 0:H], T2[0])
-            VR[:, 0:H] = va
-            VR[:, H:N] = dot(RT[:, H:N] - dot(va, G[...]), T2[1])
-            sendR[...] = dot(VR[...], VX[...])
-
-            @pl.when(e)
-            def _():
-                r_copy(k, peer).start()
+        @pl.when(k == levels)
+        def _():
+            take_rhs(kp, prev, k >= 1)
 
         @pl.when((k == levels) & e_prev)
         def _():
@@ -486,11 +498,13 @@
 
     lax.fori_loop(0, levels + 1, step, 1)
 
-    va = dot(RT[own_rt, 0:H], T2[0])
-    vb = dot(RT[own_rt, H:N] - dot(va, G[...]), T2[1])
-    xb = dot(vb, T2[1], NN)
-    out[:, H:N] = xb
-    out[:, 0:H] = dot(va - dot(xb, G[...], NN), T2[0], NN)
+    end = levels % 2
+    va = dot(RT[own_rt, 0:H], T2[end, 0])
+    vb = dot(RT[own_rt, H:N] - dot(va, G[end]), T2[end, 1])
+    xb = dot(vb, T2[end, 1], NN)
+    xa = dot(va - dot(xb, G[end], NN), T2[end, 0], NN)
+    out[0:H, :] = xa.T
+    out[H:N, :] = xb.T
 
 
 def solution(mesh):
@@ -511,9 +525,9 @@
         mrow = jnp.broadcast_to((both * mine)[None], (8, N))
         dma = pltpu.SemaphoreType.DMA
         vmem = pl.BlockSpec(memory_space=pltpu.VMEM)
-        xt = pl.pallas_call(
+        x = pl.pallas_call(
             functools.partial(kernel, slabs, levels),
-            out_shape=jax.ShapeDtypeStruct((T, N), F32),
+            out_shape=jax.ShapeDtypeStruct((N, T), F32),
             in_specs=[vmem] * 3,
             out_specs=vmem,
             scratch_shapes=[
@@ -529,8 +543,8 @@
                 pltpu.VMEM((M, N), F32),
                 pltpu.VMEM((10, T, T), F32),
                 pltpu.VMEM((10, T, T), F32),
+                pltpu.VMEM((2, 2, H, H), F32),
                 pltpu.VMEM((2, H, H), F32),
-                pltpu.VMEM((H, H), F32),
                 pltpu.VMEM((T, T), F32),
                 pltpu.VMEM((18, 8, T), F32),
                 pltpu.VMEM((8, N), F32),
@@ -559,8 +573,8 @@
             compiler_params=pltpu.CompilerParams(
                 collective_id=0, has_side_effects=True, vmem_limit_bytes=56 << 20
             ),
-        )(brow, sources[0].T, mrow)
-        return xt.T[None]
+        )(brow, sources[0], mrow)
+        return x[None]
 
     placed = (
         P("slab", None, "col"),

time: 254 us -> 246 us (0.969)
  Pallas kernels: 245 us -> 239 us
    pallas_call x1, Pallas kernels: 245 us -> 239 us  [on_device(): pl.pallas_call(functools.partial(kernel, slabs, levels), out_shape=jax.Sh...]
where the time goes in v4:
time: 246 us; the launch traced here: 244 us
  Pallas kernels  239 us (97%)
  local copies, waits for them, and re-layouts  3.46 us (1%)
    pallas_call x1, Pallas kernels, on_device(): pl.pallas_call(functools.partial(kernel, slabs, levels), out_shape=jax.Sh...  239 us

profile of v4, /device:TPU:31, one launch (start us, length us, event | category | flops | bytes accessed | tf_op | source)
XLA Modules:
  0.0 243.8 jit_solution(16995486502688482392)
XLA Ops:
  0.0 0.0 copy-start
  0.0 0.7 convert_bitcast_fusion
  0.7 0.1 broadcast_in_dim.6
  0.9 0.2 copy-done
  1.1 0.2 copy.5
  1.3 0.9 fusion.brow
  2.2 0.0 copy-start.1
  2.2 0.7 copy-done.1
  2.9 0.6 broadcast_in_dim.7.mrow
  3.5 238.6 %shard_map.46 = f32[512,128]{1,0:T(8,128)} custom-call(f32[256,512]{1,0:T(8,128)} %fusion.brow, f32[512,128]{1,0:T(8,128)} %bitcast.19, f32[8,512]{1,0:T(8,128)} %broadcast_in_dim.7.mrow), custom_call_target="tpu_custom_call" | custom-call | tf_op jit(solution)/shard_map/pallas_call | solution.py:528
  242.1 1.7 copy.9
  (2 shorter events, 0.0 us)
Async XLA Ops:
  0.0 1.1 copy-start
  2.2 0.7 copy-start.1

commit v5 on v4

--- a/solution.py
+++ b/solution.py
@@ -305,6 +305,12 @@
         def r_forward(level):
             return to_sib(recvR.at[level], sibR.at[level], rf_send, rf_recv.at[level])
 
+        def pass_on(p):
+            @pl.when(e_prev)
+            def _():
+                q_copy(p, kp, peer_prev).wait_recv()
+                q_forward(p, kp).start()
+
         def take(p):
             o, n = PIECES[p]
 
@@ -316,8 +322,6 @@
 
             @pl.when(e_prev)
             def _():
-                q_copy(p, kp, peer_prev).wait_recv()
-                q_forward(p, kp).start()
                 D[o : o + n] = D[o : o + n] - recvQ[kp, o : o + n]
 
             @pl.when(e_sib)
@@ -331,15 +335,23 @@
             def _():
                 q_forward(p, kp).wait_send()
 
+        pass_on(0)
+        pass_on(1)
         take(0)
+
+        def pass_on_rhs(level, stride, on):
+            there = s + sgn * stride
+
+            @pl.when(on & inside(there))
+            def _():
+                r_copy(level, there).wait_recv()
+                r_forward(level).start()
 
         def take_rhs(level, stride, on):
             there = s + sgn * stride
 
             @pl.when(on & inside(there))
             def _():
-                r_copy(level, there).wait_recv()
-                r_forward(level).start()
                 RT[...] = RT[...] + recvR[level]
 
             @pl.when(on & inside(s - sgn * stride))
@@ -381,6 +393,10 @@
                 DW[7 * h + 2] = DW[7 * h + 2] - dot(g, g)
                 W[...] = dot(g, inv, NN)
 
+                @pl.when(i == 0)
+                def _():
+                    pass_on(2)
+
             @pl.when(i == 2 * h + 1)
             def _():
                 T2[slot, h, T:H, T:H] = inv
@@ -388,6 +404,8 @@
 
             @pl.when(i == 1)
             def _():
+                pass_on(3)
+                pass_on_rhs(jnp.maximum(k - 2, 0), d // 4, k >= 2)
                 take(2)
                 ba = jnp.concatenate(
                     [
@@ -487,6 +505,7 @@
 
         @pl.when(k == levels)
         def _():
+            pass_on_rhs(kp, prev, k >= 1)
             take_rhs(kp, prev, k >= 1)
 
         @pl.when((k == levels) & e_prev)

time: 246 us -> 253 us (1.028)
  Pallas kernels: 239 us -> 247 us
    pallas_call x1, Pallas kernels: 239 us -> 247 us  [on_device(): pl.pallas_call(functools.partial(kernel, slabs, levels), out_shape=jax.Sh...]
where the time goes in v5:
time: 253 us
  Pallas kernels  247 us (98%)
  local copies, waits for them, and re-layouts  3.46 us (1%)
    pallas_call x1, Pallas kernels, on_device(): pl.pallas_call(functools.partial(kernel, slabs, levels), out_shape=jax.Sh...  247 us

profile of v5, /device:TPU:31, one launch (start us, length us, event | category | flops | bytes accessed | tf_op | source)
XLA Modules:
  0.0 252.6 jit_solution(16448126569526669754)
XLA Ops:
  0.0 0.0 copy-start
  0.0 0.7 convert_bitcast_fusion
  0.7 0.1 broadcast_in_dim.6
  0.9 0.2 copy-done
  1.1 0.2 copy.5
  1.3 0.9 fusion.brow
  2.2 0.0 copy-start.1
  2.2 0.7 copy-done.1
  2.9 0.6 broadcast_in_dim.7.mrow
  3.5 247.4 %shard_map.46 = f32[512,128]{1,0:T(8,128)} custom-call(f32[256,512]{1,0:T(8,128)} %fusion.brow, f32[512,128]{1,0:T(8,128)} %bitcast.19, f32[8,512]{1,0:T(8,128)} %broadcast_in_dim.7.mrow), custom_call_target="tpu_custom_call" | custom-call | tf_op jit(solution)/shard_map/pallas_call | solution.py:547
  250.9 1.7 copy.9
  (2 shorter events, 0.0 us)
Async XLA Ops:
  0.0 1.1 copy-start
  2.2 0.7 copy-start.1

commit v6 on v5

--- a/solution.py
+++ b/solution.py
@@ -364,6 +364,16 @@
                 r_forward(level).wait_send()
                 r_copy(level, there).wait_send()
 
+        def start_p(h):
+            @pl.when(e_prev & (k < levels))
+            def _():
+                p_copy(h, kp, peer_prev).start()
+
+        def start_rhs():
+            @pl.when(e_prev)
+            def _():
+                r_copy(kp, peer_prev).start()
+
         def rhs():
             take_rhs(jnp.maximum(k - 2, 0), d // 4, k >= 2)
 
@@ -374,9 +384,9 @@
                 VR[:, H:N] = dot(RT[:, H:N] - dot(va, G[was]), T2[was, 1])
                 sendR[...] = dot(VR[...], VX[...])
 
-                @pl.when(e_prev)
-                def _():
-                    r_copy(kp, peer_prev).start()
+                @pl.when(k == levels)
+                def _():
+                    start_rhs()
 
         def quarter(i, _):
             h = i // 2
@@ -396,6 +406,11 @@
                 @pl.when(i == 0)
                 def _():
                     pass_on(2)
+                    start_p(0)
+
+                @pl.when((i == 2) & (k < levels))
+                def _():
+                    start_rhs()
 
             @pl.when(i == 2 * h + 1)
             def _():
@@ -405,6 +420,7 @@
             @pl.when(i == 1)
             def _():
                 pass_on(3)
+                start_p(1)
                 pass_on_rhs(jnp.maximum(k - 2, 0), d // 4, k >= 2)
                 take(2)
                 ba = jnp.concatenate(
@@ -485,10 +501,6 @@
                     p_copy(h, kp, peer_prev).wait_send()
 
                 sendP[rows, :] = dot(VY[k, rows, :], VX[...])
-
-                @pl.when(e)
-                def _():
-                    p_copy(h, k, peer).start()
 
                 @pl.when(jnp.logical_not(e))
                 def _():

time: 253 us -> 278 us (1.099)
  Pallas kernels: 247 us -> 273 us
    pallas_call x1, Pallas kernels: 247 us -> 273 us  [on_device(): pl.pallas_call(functools.partial(kernel, slabs, levels), out_shape=jax.Sh...]
where the time goes in v6:
time: 278 us
  Pallas kernels  273 us (98%)
  local copies, waits for them, and re-layouts  3.46 us (1%)
    pallas_call x1, Pallas kernels, on_device(): pl.pallas_call(functools.partial(kernel, slabs, levels), out_shape=jax.Sh...  273 us

profile of v6, /device:TPU:31, one launch (start us, length us, event | category | flops | bytes accessed | tf_op | source)
XLA Modules:
  0.0 277.8 jit_solution(9936862145949018387)
XLA Ops:
  0.0 0.0 copy-start
  0.0 0.7 convert_bitcast_fusion
  0.7 0.1 broadcast_in_dim.6
  0.9 0.2 copy-done
  1.1 0.2 copy.5
  1.3 0.9 fusion.brow
  2.2 0.0 copy-start.1
  2.2 0.7 copy-done.1
  2.9 0.6 broadcast_in_dim.7.mrow
  3.5 272.6 %shard_map.46 = f32[512,128]{1,0:T(8,128)} custom-call(f32[256,512]{1,0:T(8,128)} %fusion.brow, f32[512,128]{1,0:T(8,128)} %bitcast.19, f32[8,512]{1,0:T(8,128)} %broadcast_in_dim.7.mrow), custom_call_target="tpu_custom_call" | custom-call | tf_op jit(solution)/shard_map/pallas_call | solution.py:559
  276.1 1.7 copy.9
  (2 shorter events, 0.0 us)
Async XLA Ops:
  0.0 1.1 copy-start
  2.2 0.7 copy-start.1

commit v7 on v5

--- a/solution.py
+++ b/solution.py
@@ -305,8 +305,11 @@
         def r_forward(level):
             return to_sib(recvR.at[level], sibR.at[level], rf_send, rf_recv.at[level])
 
-        def pass_on(p):
-            @pl.when(e_prev)
+        early = (k % 2 == 1) | (k == levels)
+        late = jnp.logical_not(early)
+
+        def pass_on(p, now):
+            @pl.when(e_prev & now)
             def _():
                 q_copy(p, kp, peer_prev).wait_recv()
                 q_forward(p, kp).start()
@@ -320,6 +323,8 @@
                     arrive(p // 2)
                 build(p)
 
+            pass_on(p, late)
+
             @pl.when(e_prev)
             def _():
                 D[o : o + n] = D[o : o + n] - recvQ[kp, o : o + n]
@@ -335,8 +340,8 @@
             def _():
                 q_forward(p, kp).wait_send()
 
-        pass_on(0)
-        pass_on(1)
+        pass_on(0, early)
+        pass_on(1, early)
         take(0)
 
         def pass_on_rhs(level, stride, on):
@@ -365,6 +370,7 @@
                 r_copy(level, there).wait_send()
 
         def rhs():
+            pass_on_rhs(jnp.maximum(k - 2, 0), d // 4, (k >= 2) & (k % 2 == 1))
             take_rhs(jnp.maximum(k - 2, 0), d // 4, k >= 2)
 
             @pl.when(k >= 1)
@@ -395,7 +401,7 @@
 
                 @pl.when(i == 0)
                 def _():
-                    pass_on(2)
+                    pass_on(2, early)
 
             @pl.when(i == 2 * h + 1)
             def _():
@@ -404,8 +410,8 @@
 
             @pl.when(i == 1)
             def _():
-                pass_on(3)
-                pass_on_rhs(jnp.maximum(k - 2, 0), d // 4, k >= 2)
+                pass_on(3, early)
+                pass_on_rhs(jnp.maximum(k - 2, 0), d // 4, (k >= 2) & (k % 2 == 0))
                 take(2)
                 ba = jnp.concatenate(
                     [

time: 253 us -> 257 us (1.016)
  Pallas kernels: 247 us -> 251 us
    pallas_call x1, Pallas kernels: 247 us -> 251 us  [on_device(): pl.pallas_call(functools.partial(kernel, slabs, levels), out_shape=jax.Sh...]
where the time goes in v7:
time: 257 us
  Pallas kernels  251 us (98%)
  local copies, waits for them, and re-layouts  3.46 us (1%)
    pallas_call x1, Pallas kernels, on_device(): pl.pallas_call(functools.partial(kernel, slabs, levels), out_shape=jax.Sh...  251 us

profile of v7, /device:TPU:31, one launch (start us, length us, event | category | flops | bytes accessed | tf_op | source)
XLA Modules:
  0.0 256.5 jit_solution(14479727336031328466)
XLA Ops:
  0.0 0.0 copy-start
  0.0 0.7 convert_bitcast_fusion
  0.7 0.1 broadcast_in_dim.6
  0.9 0.2 copy-done
  1.1 0.2 copy.5
  1.3 0.9 fusion.brow
  2.2 0.0 copy-start.1
  2.2 0.7 copy-done.1
  2.9 0.6 broadcast_in_dim.7.mrow
  3.5 251.4 %shard_map.46 = f32[512,128]{1,0:T(8,128)} custom-call(f32[256,512]{1,0:T(8,128)} %fusion.brow, f32[512,128]{1,0:T(8,128)} %bitcast.19, f32[8,512]{1,0:T(8,128)} %broadcast_in_dim.7.mrow), custom_call_target="tpu_custom_call" | custom-call | tf_op jit(solution)/shard_map/pallas_call | solution.py:553
  254.8 1.7 copy.9
  (2 shorter events, 0.0 us)
Async XLA Ops:
  0.0 1.1 copy-start
  2.2 0.7 copy-start.1

commit v8 on v4

--- a/solution.py
+++ b/solution.py
@@ -388,6 +388,7 @@
 
             @pl.when(i == 1)
             def _():
+                rhs()
                 take(2)
                 ba = jnp.concatenate(
                     [
@@ -403,7 +404,6 @@
                 DW[7] = DW[7] - gg[0:T, 0:T]
                 DW[8] = DW[8] - gg[T:H, 0:T]
                 DW[9] = DW[9] - gg[T:H, T:H]
-                rhs()
 
             return 0
 

time: 246 us -> 245 us (level)
  no operation moved by 1% of the time
where the time goes in v8:
time: 245 us; the launch traced here: 242 us
  Pallas kernels  237 us (97%)
  local copies, waits for them, and re-layouts  3.46 us (1%)
    pallas_call x1, Pallas kernels, on_device(): pl.pallas_call(functools.partial(kernel, slabs, levels), out_shape=jax.Sh...  237 us

profile of v8, /device:TPU:31, one launch (start us, length us, event | category | flops | bytes accessed | tf_op | source)
XLA Modules:
  0.0 241.9 jit_solution(10664672849732666163)
XLA Ops:
  0.0 0.0 copy-start
  0.0 0.7 convert_bitcast_fusion
  0.7 0.1 broadcast_in_dim.6
  0.9 0.2 copy-done
  1.1 0.2 copy.5
  1.3 0.9 fusion.brow
  2.2 0.0 copy-start.1
  2.2 0.7 copy-done.1
  2.9 0.6 broadcast_in_dim.7.mrow
  3.5 236.8 %shard_map.46 = f32[512,128]{1,0:T(8,128)} custom-call(f32[256,512]{1,0:T(8,128)} %fusion.brow, f32[512,128]{1,0:T(8,128)} %bitcast.19, f32[8,512]{1,0:T(8,128)} %broadcast_in_dim.7.mrow), custom_call_target="tpu_custom_call" | custom-call | tf_op jit(solution)/shard_map/pallas_call | solution.py:528
  240.3 1.7 copy.9
  (2 shorter events, 0.0 us)
Async XLA Ops:
  0.0 1.1 copy-start
  2.2 0.7 copy-start.1
